TPU v7x, 128 devices: a whole 4x4x4 slice. The times are simulated.
128 devices in a mesh: pipe: 2 (over core), space: 64 (over x, z, y).
Axes of the slice: x: 4, y: 4, z: 4, core: 2. Of those that a mesh axis runs over, the one named last changes fastest.
Arguments:
- saved_inputs: bfloat16 [2, 4, 16384, 512], P('pipe', None, 'space'), may hold values from -50 to 50
- project_in: bfloat16 [2, 512, 1536], P('pipe'), may hold values from -1.5 to 1.5
- project_out: bfloat16 [2, 512, 512], P('pipe'), may hold values from -0.25 to 0.25
- norm_gains: float32 [2, 512], P('pipe'), may hold values from 0.5 to 1.5
- neighbour_blocks: int32 [2, 4, 64, 2], P('pipe', None, 'space'), may hold values from 0 to 127, as said below
- cotangent: bfloat16 [4, 16384, 512], P(None, 'space'), may hold values from -6 to 6
Outputs:
- input_grads: bfloat16 [2, 4, 16384, 512], P('pipe', None, 'space')
Inputs may be any that keep to these rules, and one draw needn't show every extreme that they name: `neighbour_blocks`: entry e of patch p names block q * 2 + r of patch q, with q != p and |q - p| <= 2; a distance of 2 occurs; entries of one patch may repeat.
All inputs are finite; a program needn't handle non-finite values.
Results may differ from a plain program's by a relative error of at most 0.014.
Values may be sent and summed in bfloat16 or wider, within the bound.
A program may use at most 128 MiB of HBM per device.

v0:
```python
import functools

import jax
import jax.numpy as jnp
from jax import lax
from jax.experimental import pallas as pl
from jax.experimental.pallas import tpu as pltpu
from jax.sharding import PartitionSpec as P

HEADS = 32
HD = 16
BLK = 128
REACH = 2


epsilon = 1e-05


def shifted(x, axis, by):
    peers = lax.axis_size(axis)
    pairs = [(i, i + by) for i in range(peers) if 0 <= i + by < peers]
    return lax.ppermute(x, axis, pairs)


def normalize(points, gain_row):
    values = points.astype(jnp.float32)
    centre = jnp.mean(values, axis=-1, keepdims=True)
    spread = jnp.mean(jnp.square(values - centre), axis=-1, keepdims=True)
    inverse = lax.rsqrt(spread + epsilon)
    scaled = (values - centre) * inverse
    return (scaled, inverse, (scaled * gain_row).astype(jnp.bfloat16))


def norm_backward(grad_normed, scaled, inverse, gain_row):
    weighted = grad_normed * gain_row
    return inverse * (
        weighted
        - jnp.mean(weighted, axis=-1, keepdims=True)
        - scaled * jnp.mean(weighted * scaled, axis=-1, keepdims=True)
    )


MESH = pl.DeviceIdType.MESH
OFFSETS = [shift_by for shift_by in range(-REACH, REACH + 1) if shift_by != 0]


def attention_body(q_ref, k_ref, v_ref, g_ref, dq_ref, dk_ref, dv_ref, after_first):
    factor = HD ** (-0.5)
    group = 128
    per_group = group // HD
    nt = (((1,), (1,)), ((), ()))
    tn = (((0,), (0,)), ((), ()))
    head_of = lax.broadcasted_iota(jnp.int32, (1, group), 1) // HD
    dq_ref[...] = jnp.zeros_like(dq_ref)
    dk_ref[...] = jnp.zeros_like(dk_ref)
    dv_ref[...] = jnp.zeros_like(dv_ref)

    def head(index, carry):
        cols = pl.ds(pl.multiple_of((index // per_group) * group, group), group)
        mask = head_of == index % per_group
        q = q_ref[:, cols]
        k = k_ref[:, cols]
        v = v_ref[:, cols]
        g = g_ref[:, cols]
        qm = jnp.where(mask, q, jnp.zeros_like(q))
        km = jnp.where(mask, k, jnp.zeros_like(k))
        gm = jnp.where(mask, g, jnp.zeros_like(g))
        scores = lax.dot_general(qm, k, nt, preferred_element_type=jnp.float32) * factor
        top = jnp.max(scores, axis=-1, keepdims=True)
        exps = jnp.exp(scores - top)
        attention = exps * (1.0 / jnp.sum(exps, axis=-1, keepdims=True))
        grad_probs = lax.dot_general(gm, v, nt, preferred_element_type=jnp.float32)
        row = jnp.sum(attention * grad_probs, axis=-1, keepdims=True)
        grad_scores = (attention * (grad_probs - row) * factor).astype(jnp.bfloat16)
        dq_ref[:, cols] += jnp.dot(grad_scores, km, preferred_element_type=jnp.float32)
        dk_ref[:, cols] += lax.dot_general(grad_scores, qm, tn, preferred_element_type=jnp.float32)
        dv_ref[:, cols] += lax.dot_general(
            attention.astype(jnp.bfloat16), gm, tn, preferred_element_type=jnp.float32
        )
        return carry

    heads = q_ref.shape[1] // HD
    split = min(heads, 2 * per_group)
    lax.fori_loop(0, split, head, 0, unroll=2)
    after_first()
    lax.fori_loop(split, heads, head, 0, unroll=2)


def exchange_start(spreads, payload_refs, out_refs, send_sems, recv_sems):
    core = lax.axis_index("pipe")
    me = lax.axis_index("space")
    peers = lax.axis_size("space")
    barrier = pltpu.get_barrier_semaphore()

    def exists(shift_by):
        return (me + shift_by >= 0) & (me + shift_by < peers)

    def slot(shift_by):
        return OFFSETS.index(shift_by)

    for shift_by in OFFSETS:

        @pl.when(exists(shift_by))
        def _():
            pl.semaphore_signal(barrier, 1, device_id=(core, me + shift_by), device_id_type=MESH)

    pl.semaphore_wait(barrier, sum(jnp.where(exists(shift_by), 1, 0) for shift_by in OFFSETS))

    def describe(which, source, landing, shift_by):
        return pltpu.make_async_remote_copy(
            src_ref=source,
            dst_ref=out_refs[which].at[landing],
            send_sem=send_sems.at[which, landing],
            recv_sem=recv_sems.at[which, landing],
            device_id=(core, me + shift_by),
            device_id_type=MESH,
        )

    def arrival(which, landing):
        return describe(which, out_refs[which].at[landing], landing, OFFSETS[landing])

    direct = []
    relayed = []
    relaying = not any(spreads)
    for which, spread in enumerate(spreads):
        x_ref = payload_refs[which]
        targets = OFFSETS if spread or not relaying else [-1, 1]
        for shift_by in targets:
            source = x_ref.at[slot(shift_by)] if spread else x_ref
            copy = describe(which, source, slot(-shift_by), shift_by)
            direct.append((copy, exists(shift_by)))

            @pl.when(exists(shift_by))
            def _():
                copy.start()

        for shift_by in OFFSETS:

            @pl.when(jnp.logical_not(exists(shift_by)))
            def _():
                out_refs[which][slot(shift_by)] = jnp.zeros(
                    out_refs[which].shape[1:], out_refs[which].dtype
                )

        if relaying and not spread:
            for shift_by in (-1, 1):
                forward = describe(
                    which, out_refs[which].at[slot(-shift_by)], slot(-2 * shift_by), shift_by
                )
                relayed.append((which, shift_by, forward, exists(shift_by) & exists(-shift_by)))

    def relay():
        for which, shift_by, forward, valid in relayed:

            @pl.when(exists(-shift_by))
            def _():
                arrival(which, slot(-shift_by)).wait_recv()

        for which, shift_by, forward, valid in relayed:

            @pl.when(valid)
            def _():
                forward.start()

    def finish():
        for copy, valid in direct:

            @pl.when(valid)
            def _():
                copy.wait_send()

        for which, shift_by, forward, valid in relayed:

            @pl.when(valid)
            def _():
                forward.wait_send()

        relayed_slots = {(which, slot(-shift_by)) for which, shift_by, _, _ in relayed}
        for which in range(len(spreads)):
            for landing, shift_by in enumerate(OFFSETS):
                if (which, landing) in relayed_slots:
                    continue

                @pl.when(exists(shift_by))
                def _():
                    arrival(which, landing).wait_recv()

    return relay, finish


def fused_kernel(spreads, with_attention, *refs):
    count = len(spreads)
    inputs = 4 if with_attention else 0
    outputs = 3 if with_attention else 0
    attention_in = refs[:inputs]
    payload_refs = refs[inputs : inputs + count]
    attention_out = refs[inputs + count : inputs + count + outputs]
    out_refs = refs[inputs + count + outputs : inputs + 2 * count + outputs]
    send_sems, recv_sems = refs[inputs + 2 * count + outputs :]
    relay, finish = exchange_start(spreads, payload_refs, out_refs, send_sems, recv_sems)
    if with_attention:
        attention_body(*attention_in, *attention_out, relay)
    else:
        relay()
    finish()


def fused_step(attention_args, payloads, spreads, collective_id):
    vmem = pl.BlockSpec(memory_space=pltpu.VMEM)
    out_shapes = []
    flops = 0
    if attention_args:
        queries, key_rows, value_rows, grad_attn = attention_args
        rows, width = queries.shape
        keys = key_rows.shape[0]
        out_shapes = [
            jax.ShapeDtypeStruct((rows, width), jnp.float32),
            jax.ShapeDtypeStruct((keys, width), jnp.float32),
            jax.ShapeDtypeStruct((keys, width), jnp.float32),
        ]
        flops = 2 * 5 * rows * keys * width * (128 // HD)
    for payload, spread in zip(payloads, spreads):
        shape = payload.shape[1:] if spread else payload.shape
        out_shapes.append(jax.ShapeDtypeStruct((len(OFFSETS),) + shape, payload.dtype))
    moved = sum(len(OFFSETS) * x.size * x.dtype.itemsize for x in payloads)
    outs = pl.pallas_call(
        functools.partial(fused_kernel, tuple(spreads), bool(attention_args)),
        out_shape=out_shapes,
        in_specs=[vmem] * (len(attention_args) + len(payloads)),
        out_specs=[vmem] * len(out_shapes),
        scratch_shapes=[
            pltpu.SemaphoreType.DMA((len(payloads), len(OFFSETS))),
            pltpu.SemaphoreType.DMA((len(payloads), len(OFFSETS))),
        ],
        compiler_params=pltpu.CompilerParams(
            collective_id=collective_id,
            has_side_effects=True,
            vmem_limit_bytes=48 * 1024 * 1024,
        ),
        cost_estimate=pl.CostEstimate(
            flops=flops, transcendentals=flops // 160, bytes_accessed=moved + 1
        ),
    )(*attention_args, *payloads)
    return list(outs)


def swap_cores(value):
    return lax.ppermute(value, "pipe", [(0, 1), (1, 0)])


def pick(own, other, core, section):
    return jnp.where(core == section, own, other)


def prepare(rows, lists, weight_in, gain_row, myself):
    points, model_width = rows.shape
    block_count = points // BLK
    scaled, inverse, normed = normalize(rows, gain_row)
    projected = jnp.dot(normed, weight_in, preferred_element_type=jnp.float32).astype(jnp.bfloat16)
    owners = lists // block_count
    within = lists % block_count
    distance = owners - myself
    slot = jnp.where(distance < 0, distance + REACH, distance + REACH - 1)
    window_at = slot * block_count + within
    return dict(
        scaled=scaled,
        inverse=inverse,
        normed=normed,
        queries=projected[:, :model_width],
        own_pairs=projected[:, model_width:],
        window_at=window_at,
    )


def attach(unit, received, weight_in):
    points, model_width = unit["queries"].shape
    received = received.reshape(len(OFFSETS) * (points // BLK), BLK, model_width)
    fetched = jnp.take(received, unit["window_at"], axis=0).reshape(-1, model_width)
    fetched_pairs = jnp.dot(
        fetched, weight_in[:, model_width:], preferred_element_type=jnp.float32
    ).astype(jnp.bfloat16)
    unit["pairs"] = jnp.concatenate([unit["own_pairs"], fetched_pairs], 0)


def outgoing(unit, grad_key, grad_value, weight_in):
    points, model_width = unit["queries"].shape
    block_count = points // BLK
    grad_pairs = jnp.concatenate([grad_key, grad_value], 1)
    grad_remote = jnp.dot(
        grad_pairs[points:].astype(jnp.bfloat16),
        weight_in[:, model_width:].T,
        preferred_element_type=jnp.float32,
    ).reshape(-1, BLK, model_width)
    slots = lax.broadcasted_iota(jnp.int32, (len(OFFSETS) * block_count, 1, 1), 0)
    window_grads = sum(
        jnp.where(slots == unit["window_at"][entry], grad_remote[entry][None], 0.0)
        for entry in range(grad_remote.shape[0])
    )
    unit["own_grad"] = grad_pairs[:points]
    return window_grads.astype(jnp.bfloat16).reshape(len(OFFSETS), points, model_width)


def complete(unit, grad_out, grad_query, returned, weight_in, gain_row):
    grad_project = jnp.concatenate([grad_query, unit["own_grad"]], 1).astype(jnp.bfloat16)
    grad_normed = jnp.dot(grad_project, weight_in.T, preferred_element_type=jnp.float32)
    grad_normed = grad_normed + jnp.sum(returned.astype(jnp.float32), axis=0)
    return (
        grad_out.astype(jnp.float32)
        + norm_backward(grad_normed, unit["scaled"], unit["inverse"], gain_row)
    ).astype(jnp.bfloat16)


def shards(saved_inputs, project_in, project_out, norm_gains, neighbour_blocks, cotangent):
    sections = lax.axis_size("pipe")
    core = lax.axis_index("pipe")
    other = sections - 1 - core
    myself = lax.axis_index("space")
    micro_count = cotangent.shape[0]
    half = micro_count // sections
    model_width = cotangent.shape[2]

    def mine(array, whose):
        grouped = array.reshape((half, sections) + array.shape[1:])
        return lax.dynamic_index_in_dim(grouped, whose, 1, keepdims=False)

    local_lists = neighbour_blocks[0, :, 0, :]
    own = (
        mine(saved_inputs[0], core),
        mine(local_lists, core),
        project_in[0],
        project_out[0],
        norm_gains[0],
    )
    got = swap_cores(
        (
            mine(saved_inputs[0], other),
            mine(local_lists, other),
            project_in[0],
            project_out[0],
            norm_gains[0],
        )
    )
    params = [
        [pick(own_part, got_part, core, section) for own_part, got_part in zip(own, got)]
        for section in range(sections)
    ]
    cotangent_mine = mine(cotangent, core)
    order = [(section, j) for section in range(sections - 1, -1, -1) for j in range(half)]
    units = [
        prepare(params[section][0][j], params[section][1][j], params[section][2], params[section][4], myself)
        for section, j in order
    ]
    results = {}
    exchanged = {}
    ids = iter(range(len(order) + 2))
    (first_received,) = fused_step((), [units[0]["normed"]], [False], next(ids))
    attach(units[0], first_received, params[order[0][0]][2])
    pending = None
    for step, (section, j) in enumerate(order):
        unit = units[step]
        _, _, weight_in, weight_out, gain_row = params[section]
        grad_out = cotangent_mine[j] if section == sections - 1 else results[(section + 1, j)]
        unit["grad_out"] = grad_out
        grad_attn = jnp.dot(grad_out, weight_out.T, preferred_element_type=jnp.float32).astype(
            jnp.bfloat16
        )
        payloads, spreads = [], []
        if pending is not None:
            payloads.append(pending[1])
            spreads.append(True)
        if step == 0:
            for later in units[1:]:
                payloads.append(later["normed"])
                spreads.append(False)
        outs = fused_step(
            (unit["queries"], unit["pairs"][:, :model_width], unit["pairs"][:, model_width:], grad_attn),
            payloads,
            spreads,
            next(ids),
        )
        grad_query, grad_key, grad_value = outs[:3]
        received = outs[3:]
        if pending is not None:
            done_step, _ = pending
            done_section, done_j = order[done_step]
            done_unit = units[done_step]
            results[(done_section, done_j)] = complete(
                done_unit,
                done_unit["grad_out"],
                done_unit["grad_query"],
                received[0],
                params[done_section][2],
                params[done_section][4],
            )
            exchanged[(done_section, done_j)] = swap_cores(results[(done_section, done_j)])
            received = received[1:]
        if step == 0:
            for later, (later_section, _), arrived in zip(units[1:], order[1:], received):
                attach(later, arrived, params[later_section][2])
        unit["grad_query"] = grad_query
        pending = (step, outgoing(unit, grad_key, grad_value, weight_in))
    done_step, window = pending
    done_section, done_j = order[done_step]
    done_unit = units[done_step]
    (returned,) = fused_step((), [window], [True], next(ids))
    results[(done_section, done_j)] = complete(
        done_unit,
        done_unit["grad_out"],
        done_unit["grad_query"],
        returned,
        params[done_section][2],
        params[done_section][4],
    )
    exchanged[(done_section, done_j)] = swap_cores(results[(done_section, done_j)])
    own_out = jnp.stack([pick(results[(0, j)], results[(1, j)], core, 0) for j in range(half)])
    other_out = jnp.stack(
        [pick(exchanged[(0, j)], exchanged[(1, j)], core, 0) for j in range(half)]
    )
    grouped = jnp.stack([pick(own_out, other_out, core, parity) for parity in range(sections)], 1)
    return grouped.reshape((1, micro_count) + grouped.shape[2:])


def solution(mesh):
    return jax.shard_map(
        shards,
        mesh=mesh,
        in_specs=(
            P("pipe", None, "space", None),
            P("pipe", None, None),
            P("pipe", None, None),
            P("pipe", None),
            P("pipe", None, "space", None),
            P(None, "space", None),
        ),
        out_specs=P("pipe", None, "space", None),
        check_vma=False,
    )
```

profile of v0, /device:TPU:15, one launch (start us, length us, event | category | flops | bytes accessed | tf_op | source)
XLA Modules:
  0.0 243.1 jit_solution(17970503163711935537)
XLA Ops:
  0.0 0.8 reshape_squeeze.9
  1.0 0.7 collective-permute-start.3
  1.8 1.1 dynamic-slice_bitcast_fusion
  2.9 0.5 collective-permute-start
  4.0 0.7 fusion.137
  4.7 0.7 fusion.135
  5.4 0.7 fusion.103
  6.1 0.6 fusion.102
  6.8 0.6 fusion.104
  7.5 0.7 fusion.105
  8.3 0.6 fusion.99
  8.9 0.7 fusion.98
  9.7 0.6 fusion.100
  10.4 0.6 fusion.101
  11.1 0.7 broadcast_select_fusion.15
  13.1 20.0 %shard_map.64 = bf16[4,256,512]{2,1,0:T(8,128)(2,1)S(1)} custom-call(bf16[256,512]{1,0:T(8,128)(2,1)S(1)} %get-tuple-element.87.refs_0_), custom_call_target="tpu_custom_call" | custom-call | bytes 1048577 | tf_op jit(solution)/shard_map/pallas_call | solution.py:226
  33.1 0.6 gather_fusion
  34.1 0.7 copy-done.24
  35.4 0.7 copy-done.20
  36.1 1.6 broadcast_select_fusion.1
  37.8 0.6 convolution_convert_fusion.3
  38.4 0.6 convolution_convert_fusion.2
  39.0 0.7 copy-done.12
  39.7 0.6 convolution_convert_fusion
  40.6 0.6 convolution_convert_fusion.1
  41.5 0.9 copy-done.15
  43.0 39.9 %shard_map.65 = (f32[256,512]{1,0:T(8,128)S(1)}, f32[512,512]{1,0:T(8,128)S(1)}, f32[512,512]{1,0:T(8,128)S(1)}, bf16[4,256,512]{2,1,0:T(8,128)(2,1)S(1)}, bf16[...) custom-call(bf16[256,512]{1,0:T(8,128)(2,1)S(1)} %slice.241.refs_0_, ...), custom_call_target="tpu_custom_call" | custom-call | flops 5368709120 | bytes 3145729 | tf_op jit(solution)/shard_map/pallas_call | solution.py:226
  83.0 1.3 fusion.32
  84.2 0.6 gather_fusion.1
  84.9 1.7 convolution_convert_fusion.6
  86.6 1.1 fusion.134
  88.3 1.2 fusion.7.refs_4_
  89.6 31.2 %shard_map.66 = (f32[256,512]{1,0:T(8,128)S(1)}, f32[512,512]{1,0:T(8,128)S(1)}, f32[512,512]{1,0:T(8,128)S(1)}, bf16[4,256,512]{2,1,0:T(8,128)(2,1)S(1)}) custom-call(bf16[256,512]{1,0:T(8,128)(2,1)S(1)} %slice.250.refs_0_, bf16[512,512]{1,0:T(8,128)(2,1)S(1)} %get-tuple-element.79.refs_1_, bf16[512,512]{1,0:T(8,128)(2,1)S(1)} %get-tuple-element.78.refs_2_, ...), custom_call_target="tpu_custom_call" | custom-call | flops 5368709120 | bytes 4194305 | tf_op jit(solution)/shard_map/pallas_call | solution.py:226
  120.9 1.6 copy-done.4
  122.5 1.3 fusion.30
  123.8 1.8 gather_fusion.2
  125.8 1.8 convolution_convert_fusion.5
  127.8 0.7 fusion.124
  128.5 1.3 fusion.47
  129.8 5.9 %collective-permute-start.6 = (bf16[256,512]{1,0:T(8,128)(2,1)S(1)}, bf16[256,512]{1,0:T(8,128)(2,1)}, u32[]{:S(2)}, u32[]{:S(2)}) collective-permute-start(bf16[256,512]{1,0:T(8,128)(2,1)S(1)} %fusion.47), channel_id=1, source_target_pairs={{0,64},{64,0},{1,65},{65,1},{2,66},{66,2},{3,67},{67,3},{4,68},{68... | collective-permute-start | bytes 786440 | tf_op jit(solution)/shard_map/ppermute | solution.py:248
  136.4 1.2 fusion.5.refs_4_
  137.6 1.4 convolution_convert_fusion.9.refs_3_
  139.0 28.7 %shard_map.67 = (f32[256,512]{1,0:T(8,128)S(1)}, f32[512,512]{1,0:T(8,128)S(1)}, f32[512,512]{1,0:T(8,128)S(1)}, bf16[4,256,512]{2,1,0:T(8,128)(2,1)S(1)}) custom-call(bf16[256,512]{1,0:T(8,128)(2,1)S(1)} %slice.257.refs_0_, bf16[512,512]{1,0:T(8,128)(2,1)S(1)} %get-tuple-element.81.refs_1_, bf16[512,512]{1,0:T(8,128)(2,1)S(1)} %get-tuple-element.80.refs_2_, ...), custom_call_target="tpu_custom_call" | custom-call | flops 5368709120 | bytes 4194305 | tf_op jit(solution)/shard_map/pallas_call | solution.py:226
  167.9 1.3 copy-done.1
  169.1 0.5 fusion.26
  169.6 0.5 copy-done.18
  170.1 1.8 gather_fusion.3
  172.0 1.7 convolution_convert_fusion.4
  174.0 1.2 copy-done.6
  175.3 0.7 fusion.123
  176.4 1.2 fusion.60
  178.2 1.2 fusion.3.refs_4_
  179.4 1.4 convolution_convert_fusion.8.refs_3_
  180.8 30.1 %shard_map.68 = (f32[256,512]{1,0:T(8,128)S(1)}, f32[512,512]{1,0:T(8,128)S(1)}, f32[512,512]{1,0:T(8,128)S(1)}, bf16[4,256,512]{2,1,0:T(8,128)(2,1)S(1)}) custom-call(bf16[256,512]{1,0:T(8,128)(2,1)S(1)} %slice.266.refs_0_, bf16[512,512]{1,0:T(8,128)(2,1)S(1)} %get-tuple-element.77.refs_1_, bf16[512,512]{1,0:T(8,128)(2,1)S(1)} %get-tuple-element.76.refs_2_, ...), custom_call_target="tpu_custom_call" | custom-call | flops 5368709120 | bytes 4194305 | tf_op jit(solution)/shard_map/pallas_call | solution.py:226
  211.1 1.3 copy-done.2
  212.8 0.5 copy-done.19
  214.6 21.8 %shard_map.69 = bf16[4,256,512]{2,1,0:T(8,128)(2,1)S(1)} custom-call(bf16[4,256,512]{2,1,0:T(8,128)(2,1)S(1)} %fusion.1.refs_0_), custom_call_target="tpu_custom_call" | custom-call | bytes 4194305 | tf_op jit(solution)/shard_map/pallas_call | solution.py:226
  236.6 0.6 fusion.8
  237.8 0.8 fusion.122
  238.6 0.7 select_bitcast_fusion.3
  239.4 0.5 collective-permute-start.8
  240.0 0.9 collective-permute-done.5
  240.9 1.0 select_bitcast_fusion.1
  242.1 1.1 pad_maximum_fusion
  (157 shorter events, 11.2 us)
Async XLA Ops:
  0.0 11.8 %copy-start.21 = (bf16[1,4,256,512]{3,2,1,0:T(8,128)(2,1)S(1)}, bf16[1,4,256,512]{3,2,1,0:T(8,128)(2,1)}, u32[]{:S(2)}) copy-start(bf16[1,4,256,512]{3,2,1,0:T(8,128)(2,1)} %param.8) | copy-start | bytes 3145732
  1.0 3.0 %collective-permute-start.3 = (s32[2,2]{1,0:T(2,128)S(1)}, s32[2,2]{1,0:T(2,128)S(1)}, u32[]{:S(2)}, u32[]{:S(2)}) collective-permute-start(s32[2,2]{1,0:T(2,128)S(1)} %bitcast.350), channel_id=1, source_target_pairs={{0,64},{64,0},{1,65},{65,1},{2,66},{66,2},{3,67},{67,3},{4,68},{68... | collective-permute-start | bytes 56 | tf_op jit(solution)/shard_map/ppermute | solution.py:248
  1.7 9.4 %collective-permute-start.1 = (f32[512]{0:T(512)}, f32[512]{0:T(512)S(1)}, u32[]{:S(2)}, u32[]{:S(2)}) collective-permute-start(f32[512]{0:T(512)} %bitcast.348), channel_id=1, source_target_pairs={{0,64},{64,0},{1,65},{65,1},{2,66},{66,2},{3,67},{67,3},{4,68},{68... | collective-permute-start | bytes 6152 | tf_op jit(solution)/shard_map/ppermute | solution.py:248
  2.9 8.9 %collective-permute-start = (bf16[2,256,512]{2,1,0:T(8,128)(2,1)S(1)}, bf16[2,256,512]{2,1,0:T(8,128)(2,1)S(1)}, u32[]{:S(2)}, u32[]{:S(2)}) collective-permute-start(bf16[2,256,512]{2,1,0:T(8,128)(2,1)S(1)} %dynamic-slice_bitcast_fusion), channel_id=1, source_target_pairs={{0,64},{64,0},{1,65},{65,1},{2,66},{66,2},{3,67},{67,3},{4,68},{68... | collective-permute-start | bytes 1572872 | tf_op jit(solution)/shard_map/ppermute | solution.py:248
  3.4 30.7 %collective-permute-start.4 = (bf16[512,512]{1,0:T(8,128)(2,1)}, bf16[512,512]{1,0:T(8,128)(2,1)}, u32[]{:S(2)}, u32[]{:S(2)}) collective-permute-start(bf16[512,512]{1,0:T(8,128)(2,1)} %bitcast.351), channel_id=1, source_target_pairs={{0,64},{64,0},{1,65},{65,1},{2,66},{66,2},{3,67},{67,3},{4,68},{68... | collective-permute-start | bytes 1572872 | tf_op jit(solution)/shard_map/ppermute | solution.py:248
  3.5 32.0 %collective-permute-start.2 = (bf16[512,1536]{1,0:T(8,128)(2,1)}, bf16[512,1536]{1,0:T(8,128)(2,1)}, u32[]{:S(2)}, u32[]{:S(2)}) collective-permute-start(bf16[512,1536]{1,0:T(8,128)(2,1)} %bitcast.335), channel_id=1, source_target_pairs={{0,64},{64,0},{1,65},{65,1},{2,66},{66,2},{3,67},{67,3},{4,68},{68... | collective-permute-start | bytes 4718600 | tf_op jit(solution)/shard_map/ppermute | solution.py:248
  11.9 1.2 copy-start.7
  11.9 21.9 %copy-start.10 = (bf16[2,256,512]{2,1,0:T(8,128)(2,1)}, bf16[2,256,512]{2,1,0:T(8,128)(2,1)S(1)}, u32[]{:S(2)}) copy-start(bf16[2,256,512]{2,1,0:T(8,128)(2,1)S(1)} %get-tuple-element.73) | copy-start | bytes 1572868
  13.1 21.0 %copy-start.23 = (bf16[4,256,512]{2,1,0:T(8,128)(2,1)S(1)}, bf16[4,256,512]{2,1,0:T(8,128)(2,1)}, u32[]{:S(2)}) copy-start(bf16[4,256,512]{2,1,0:T(8,128)(2,1)} %param.13) | copy-start | bytes 3145732
  33.7 1.0 copy-start.24
  34.7 1.4 copy-start.20
  37.8 2.8 %copy-start = (bf16[512,1536]{1,0:T(8,128)(2,1)}, bf16[512,1536]{1,0:T(8,128)(2,1)S(1)}, u32[]{:S(2)}) copy-start(bf16[512,1536]{1,0:T(8,128)(2,1)S(1)} %get-tuple-element.71) | copy-start | bytes 4718596
  37.8 45.2 %copy-start.3 = (bf16[512,1536]{1,0:T(8,128)(2,1)}, bf16[512,1536]{1,0:T(8,128)(2,1)S(1)}, u32[]{:S(2)}) copy-start(bf16[512,1536]{1,0:T(8,128)(2,1)S(1)} %get-tuple-element.70) | copy-start | bytes 4718596
  38.3 1.3 copy-start.12
  39.7 0.9 copy-start.13
  40.6 0.9 copy-start.14
  41.5 0.9 copy-start.15
  41.5 1.4 slice-start
  83.0 1.3 copy-start.16
  84.9 2.8 %slice-start.1 = ((bf16[256,1536]{1,0:T(8,128)(2,1)}), bf16[256,1024]{1,0:T(8,128)(2,1)S(1)}, s32[]{:S(2)}) async-start(bf16[256,1536]{1,0:T(8,128)(2,1)} %copy-done.13), calls=%async_computation.1 | async-start | bytes 1048576 | tf_op jit(solution)/shard_map/slice | solution.py:270
  120.8 1.8 copy-start.4
  120.9 2.9 %copy-start.17 = (bf16[512,1024]{1,0:T(8,128)(2,1)}, bf16[512,1024]{1,0:T(8,128)(2,1)S(1)}, u32[]{:S(2)}) copy-start(bf16[512,1024]{1,0:T(8,128)(2,1)S(1)} %maximum_convert_fusion.1) | copy-start | bytes 3145732
  125.7 2.0 copy-start.5
  125.7 2.0 copy-start.8
  125.8 2.0 slice-start.4
  128.5 7.2 %copy-start.22 = (f32[256,512]{1,0:T(8,128)S(1)}, f32[256,512]{1,0:T(8,128)}, u32[]{:S(2)}) copy-start(f32[256,512]{1,0:T(8,128)} %fusion.30) | copy-start | bytes 1572868
  128.5 7.2 %slice-start.3 = ((bf16[256,1536]{1,0:T(8,128)(2,1)}), bf16[256,1024]{1,0:T(8,128)(2,1)S(1)}, s32[]{:S(2)}) async-start(bf16[256,1536]{1,0:T(8,128)(2,1)} %copy-done.15), calls=%async_computation.3 | async-start | bytes 1048576 | tf_op jit(solution)/shard_map/slice | solution.py:270
  129.8 110.2 %collective-permute-start.6 = (bf16[256,512]{1,0:T(8,128)(2,1)S(1)}, bf16[256,512]{1,0:T(8,128)(2,1)}, u32[]{:S(2)}, u32[]{:S(2)}) collective-permute-start(bf16[256,512]{1,0:T(8,128)(2,1)S(1)} %fusion.47), channel_id=1, source_target_pairs={{0,64},{64,0},{1,65},{65,1},{2,66},{66,2},{3,67},{67,3},{4,68},{68... | collective-permute-start | bytes 786440 | tf_op jit(solution)/shard_map/ppermute | solution.py:248
  136.4 1.3 copy-start.25
  167.7 1.4 copy-start.1
  169.1 1.0 copy-start.18
  172.0 2.0 slice-start.5
  173.8 1.4 copy-start.6
  173.8 1.5 copy-start.9
  175.3 1.0 slice-start.2
  178.1 1.3 copy-start.26
  210.9 1.4 copy-start.2
  212.3 1.0 copy-start.19
  214.6 22.0 %slice-start.7 = ((bf16[512,1024]{1,0:T(8,128)(2,1)}), bf16[256,1024]{1,0:T(8,128)(2,1)S(1)}, s32[]{:S(2)}) async-start(bf16[512,1024]{1,0:T(8,128)(2,1)} %copy-done.19), calls=%async_computation.7 | async-start | bytes 1048576 | tf_op jit(solution)/shard_map/slice | solution.py:299
  236.6 1.0 copy-start.11
  236.6 1.2 slice-start.6
  239.3 1.6 collective-permute-start.5
  239.4 2.5 %collective-permute-start.8 = (bf16[256,512]{1,0:T(8,128)(2,1)S(1)}, bf16[256,512]{1,0:T(8,128)(2,1)S(1)}, u32[]{:S(2)}, u32[]{:S(2)}) collective-permute-start(bf16[256,512]{1,0:T(8,128)(2,1)S(1)} %fusion.60), channel_id=1, source_target_pairs={{0,64},{64,0},{1,65},{65,1},{2,66},{66,2},{3,67},{67,3},{4,68},{68... | collective-permute-start | bytes 786440 | tf_op jit(solution)/shard_map/ppermute | solution.py:248
  239.9 2.0 collective-permute-start.7
where the time goes:
time: 245 us; the launch traced here: 243 us
  Pallas kernels  172 us (70%)
  local copies, waits for them, and re-layouts  23.1 us (9%)
  other arithmetic  20.3 us (8%)
  matrix products  17.7 us (7%)
  starting transfers between devices  8.32 us (3%)
    pallas_call x6, Pallas kernels, fused_step(): pl.pallas_call(functools.partial(fused_kernel, tuple(spreads), bool(atten...  172 us
    unnamed x54, local copies, waits for them, and re-layouts  10.5 us
    ppermute x9, starting transfers between devices, swap_cores(): return lax.ppermute(value, 'pipe', [(0, 1), (1, 0)])  8.32 us
    dot_general x4, matrix products, attach(): jnp.dot(fetched, weight_in[:, model_width:], preferred_element_type=jnp.f...  5.69 us
    eq x8, other arithmetic, outgoing(): slots == unit['window_at'][entry]  5.03 us
  transfers between devices with their start and end apart: 9, of which 1 were waited for; matrix products, arithmetic and copies ran while one was open for 12% of the time, Pallas kernels for 41%

commit v1 on v0

--- a/solution.py
+++ b/solution.py
@@ -351,7 +351,6 @@
         for section, j in order
     ]
     results = {}
-    exchanged = {}
     ids = iter(range(len(order) + 2))
     (first_received,) = fused_step((), [units[0]["normed"]], [False], next(ids))
     attach(units[0], first_received, params[order[0][0]][2])
@@ -392,7 +391,6 @@
                 params[done_section][2],
                 params[done_section][4],
             )
-            exchanged[(done_section, done_j)] = swap_cores(results[(done_section, done_j)])
             received = received[1:]
         if step == 0:
             for later, (later_section, _), arrived in zip(units[1:], order[1:], received):
@@ -411,10 +409,9 @@
         params[done_section][2],
         params[done_section][4],
     )
-    exchanged[(done_section, done_j)] = swap_cores(results[(done_section, done_j)])
     own_out = jnp.stack([pick(results[(0, j)], results[(1, j)], core, 0) for j in range(half)])
-    other_out = jnp.stack(
-        [pick(exchanged[(0, j)], exchanged[(1, j)], core, 0) for j in range(half)]
+    other_out = swap_cores(
+        jnp.stack([pick(results[(1, j)], results[(0, j)], core, 0) for j in range(half)])
     )
     grouped = jnp.stack([pick(own_out, other_out, core, parity) for parity in range(sections)], 1)
     return grouped.reshape((1, micro_count) + grouped.shape[2:])

time: 245 us -> 240 us (0.980)
  Pallas kernels: 172 us -> 168 us
  starting transfers between devices: 8.32 us -> 5.41 us
    pallas_call x6, Pallas kernels: 172 us -> 168 us  [fused_step(): pl.pallas_call(functools.partial(fused_kernel, tuple(spreads), bool(atten...]
    ppermute x9 -> x6, starting transfers between devices: 8.32 us -> 5.41 us  [swap_cores(): return lax.ppermute(value, 'pipe', [(0, 1), (1, 0)])]
  transfers between devices with their start and end apart: 9 -> 6, of which waited for: 1 -> 1; matrix products, arithmetic and copies ran while one was open for 12% -> 5% of each run, Pallas kernels for 41% -> 8%
where the time goes in v1:
time: 240 us; the launch traced here: 236 us
  Pallas kernels  168 us (70%)
  local copies, waits for them, and re-layouts  24.4 us (10%)
  other arithmetic  18.4 us (8%)
  matrix products  17.7 us (7%)
  starting transfers between devices  5.41 us (2%)
    pallas_call x6, Pallas kernels, fused_step(): pl.pallas_call(functools.partial(fused_kernel, tuple(spreads), bool(atten...  168 us
    unnamed x54, local copies, waits for them, and re-layouts  10.8 us
    dot_general x4, matrix products, attach(): jnp.dot(fetched, weight_in[:, model_width:], preferred_element_type=jnp.f...  5.69 us
    ppermute x6, starting transfers between devices, swap_cores(): return lax.ppermute(value, 'pipe', [(0, 1), (1, 0)])  5.41 us
    eq x8, other arithmetic, outgoing(): slots == unit['window_at'][entry]  5.06 us
  transfers between devices with their start and end apart: 6, of which 1 were waited for; matrix products, arithmetic and copies ran while one was open for 5% of the time, Pallas kernels for 8%

profile of v1, /device:TPU:15, one launch (start us, length us, event | category | flops | bytes accessed | tf_op | source)
XLA Modules:
  0.0 236.4 jit_solution(6831548283082192070)
XLA Ops:
  0.0 0.8 reshape_squeeze.9
  1.0 0.7 collective-permute-start.3
  1.8 1.1 dynamic-slice_bitcast_fusion
  2.9 0.5 collective-permute-start
  4.0 0.7 fusion.137
  4.7 0.7 fusion.135
  5.4 0.7 fusion.103
  6.1 0.6 fusion.102
  6.8 0.6 fusion.104
  7.6 0.6 fusion.105
  8.3 0.6 fusion.99
  9.0 0.6 fusion.98
  9.7 0.7 fusion.100
  10.4 0.6 fusion.101
  11.1 0.7 broadcast_select_fusion.13
  13.1 20.0 %shard_map.64 = bf16[4,256,512]{2,1,0:T(8,128)(2,1)S(1)} custom-call(bf16[256,512]{1,0:T(8,128)(2,1)S(1)} %get-tuple-element.87.refs_0_), custom_call_target="tpu_custom_call" | custom-call | bytes 1048577 | tf_op jit(solution)/shard_map/pallas_call | solution.py:226
  33.1 0.6 gather_fusion
  34.1 0.7 copy-done.24
  35.5 0.7 copy-done.20
  36.2 1.6 broadcast_select_fusion.1
  37.8 0.6 convolution_convert_fusion.3
  38.4 0.6 convolution_convert_fusion.2
  39.0 0.7 copy-done.12
  39.7 0.6 convolution_convert_fusion
  40.6 0.6 convolution_convert_fusion.1
  41.5 0.9 copy-done.15
  43.0 39.8 %shard_map.65 = (f32[256,512]{1,0:T(8,128)S(1)}, f32[512,512]{1,0:T(8,128)S(1)}, f32[512,512]{1,0:T(8,128)S(1)}, bf16[4,256,512]{2,1,0:T(8,128)(2,1)S(1)}, bf16[...) custom-call(bf16[256,512]{1,0:T(8,128)(2,1)S(1)} %slice.241.refs_0_, ...), custom_call_target="tpu_custom_call" | custom-call | flops 5368709120 | bytes 3145729 | tf_op jit(solution)/shard_map/pallas_call | solution.py:226
  83.0 1.3 fusion.32
  84.2 0.6 gather_fusion.1
  84.9 1.7 convolution_convert_fusion.6
  86.6 1.1 fusion.134
  88.3 1.2 fusion.7.refs_4_
  89.6 31.2 %shard_map.66 = (f32[256,512]{1,0:T(8,128)S(1)}, f32[512,512]{1,0:T(8,128)S(1)}, f32[512,512]{1,0:T(8,128)S(1)}, bf16[4,256,512]{2,1,0:T(8,128)(2,1)S(1)}) custom-call(bf16[256,512]{1,0:T(8,128)(2,1)S(1)} %slice.250.refs_0_, bf16[512,512]{1,0:T(8,128)(2,1)S(1)} %get-tuple-element.79.refs_1_, bf16[512,512]{1,0:T(8,128)(2,1)S(1)} %get-tuple-element.78.refs_2_, ...), custom_call_target="tpu_custom_call" | custom-call | flops 5368709120 | bytes 4194305 | tf_op jit(solution)/shard_map/pallas_call | solution.py:226
  120.9 1.6 copy-done.4
  122.5 1.3 fusion.30
  123.8 1.8 gather_fusion.2
  125.7 1.8 convolution_convert_fusion.5
  127.8 0.7 fusion.124
  129.0 1.2 fusion.47
  130.8 1.2 fusion.5.refs_4_
  132.0 1.4 convolution_convert_fusion.9.refs_3_
  133.4 30.1 %shard_map.67 = (f32[256,512]{1,0:T(8,128)S(1)}, f32[512,512]{1,0:T(8,128)S(1)}, f32[512,512]{1,0:T(8,128)S(1)}, bf16[4,256,512]{2,1,0:T(8,128)(2,1)S(1)}) custom-call(bf16[256,512]{1,0:T(8,128)(2,1)S(1)} %slice.257.refs_0_, bf16[512,512]{1,0:T(8,128)(2,1)S(1)} %get-tuple-element.81.refs_1_, bf16[512,512]{1,0:T(8,128)(2,1)S(1)} %get-tuple-element.80.refs_2_, ...), custom_call_target="tpu_custom_call" | custom-call | flops 5368709120 | bytes 4194305 | tf_op jit(solution)/shard_map/pallas_call | solution.py:226
  163.6 1.3 copy-done.1
  164.9 0.5 fusion.26
  165.4 0.5 copy-done.18
  165.9 1.8 gather_fusion.3
  167.8 1.7 convolution_convert_fusion.4
  169.7 1.2 copy-done.6
  171.0 0.7 fusion.123
  172.1 1.2 fusion.60
  173.9 1.2 fusion.3.refs_4_
  175.1 1.4 convolution_convert_fusion.8.refs_3_
  176.5 28.8 %shard_map.68 = (f32[256,512]{1,0:T(8,128)S(1)}, f32[512,512]{1,0:T(8,128)S(1)}, f32[512,512]{1,0:T(8,128)S(1)}, bf16[4,256,512]{2,1,0:T(8,128)(2,1)S(1)}) custom-call(bf16[256,512]{1,0:T(8,128)(2,1)S(1)} %slice.266.refs_0_, bf16[512,512]{1,0:T(8,128)(2,1)S(1)} %get-tuple-element.77.refs_1_, bf16[512,512]{1,0:T(8,128)(2,1)S(1)} %get-tuple-element.76.refs_2_, ...), custom_call_target="tpu_custom_call" | custom-call | flops 5368709120 | bytes 4194305 | tf_op jit(solution)/shard_map/pallas_call | solution.py:226
  205.5 1.3 copy-done.2
  206.7 0.5 fusion.24
  207.2 0.5 copy-done.19
  208.5 0.5 fusion.1.refs_0_
  209.0 18.0 %shard_map.69 = bf16[4,256,512]{2,1,0:T(8,128)(2,1)S(1)} custom-call(bf16[4,256,512]{2,1,0:T(8,128)(2,1)S(1)} %fusion.1.refs_0_), custom_call_target="tpu_custom_call" | custom-call | bytes 4194305 | tf_op jit(solution)/shard_map/pallas_call | solution.py:226
  227.2 0.6 fusion.8
  228.3 0.8 fusion.122
  229.2 0.7 select_bitcast_fusion.5
  230.0 3.6 %collective-permute-start.5 = (bf16[2,256,512]{2,1,0:T(8,128)(2,1)S(1)}, bf16[2,256,512]{2,1,0:T(8,128)(2,1)S(1)}, u32[]{:S(2)}, u32[]{:S(2)}) collective-permute-start(bf16[2,256,512]{2,1,0:T(8,128)(2,1)S(1)} %pad_maximum_fusion.6), channel_id=1, source_target_pairs={{0,64},{64,0},{1,65},{65,1},{2,66},{66,2},{3,67},{67,3},{4,68},{68... | collective-permute-start | bytes 1572872 | tf_op jit(solution)/shard_map/ppermute | solution.py:248
  233.6 1.5 collective-permute-done.5
  235.3 1.0 copy.15
  (153 shorter events, 10.6 us)
Async XLA Ops:
  0.0 11.8 %copy-start.21 = (bf16[1,4,256,512]{3,2,1,0:T(8,128)(2,1)S(1)}, bf16[1,4,256,512]{3,2,1,0:T(8,128)(2,1)}, u32[]{:S(2)}) copy-start(bf16[1,4,256,512]{3,2,1,0:T(8,128)(2,1)} %param.8) | copy-start | bytes 3145732
  1.0 3.0 %collective-permute-start.3 = (s32[2,2]{1,0:T(2,128)S(1)}, s32[2,2]{1,0:T(2,128)S(1)}, u32[]{:S(2)}, u32[]{:S(2)}) collective-permute-start(s32[2,2]{1,0:T(2,128)S(1)} %bitcast.354), channel_id=1, source_target_pairs={{0,64},{64,0},{1,65},{65,1},{2,66},{66,2},{3,67},{67,3},{4,68},{68... | collective-permute-start | bytes 56 | tf_op jit(solution)/shard_map/ppermute | solution.py:248
  1.7 9.4 %collective-permute-start.1 = (f32[512]{0:T(512)}, f32[512]{0:T(512)S(1)}, u32[]{:S(2)}, u32[]{:S(2)}) collective-permute-start(f32[512]{0:T(512)} %bitcast.352), channel_id=1, source_target_pairs={{0,64},{64,0},{1,65},{65,1},{2,66},{66,2},{3,67},{67,3},{4,68},{68... | collective-permute-start | bytes 6152 | tf_op jit(solution)/shard_map/ppermute | solution.py:248
  2.9 9.0 %collective-permute-start = (bf16[2,256,512]{2,1,0:T(8,128)(2,1)S(1)}, bf16[2,256,512]{2,1,0:T(8,128)(2,1)S(1)}, u32[]{:S(2)}, u32[]{:S(2)}) collective-permute-start(bf16[2,256,512]{2,1,0:T(8,128)(2,1)S(1)} %dynamic-slice_bitcast_fusion), channel_id=1, source_target_pairs={{0,64},{64,0},{1,65},{65,1},{2,66},{66,2},{3,67},{67,3},{4,68},{68... | collective-permute-start | bytes 1572872 | tf_op jit(solution)/shard_map/ppermute | solution.py:248
  3.4 30.7 %collective-permute-start.4 = (bf16[512,512]{1,0:T(8,128)(2,1)}, bf16[512,512]{1,0:T(8,128)(2,1)}, u32[]{:S(2)}, u32[]{:S(2)}) collective-permute-start(bf16[512,512]{1,0:T(8,128)(2,1)} %bitcast.355), channel_id=1, source_target_pairs={{0,64},{64,0},{1,65},{65,1},{2,66},{66,2},{3,67},{67,3},{4,68},{68... | collective-permute-start | bytes 1572872 | tf_op jit(solution)/shard_map/ppermute | solution.py:248
  3.5 32.0 %collective-permute-start.2 = (bf16[512,1536]{1,0:T(8,128)(2,1)}, bf16[512,1536]{1,0:T(8,128)(2,1)}, u32[]{:S(2)}, u32[]{:S(2)}) collective-permute-start(bf16[512,1536]{1,0:T(8,128)(2,1)} %bitcast.339), channel_id=1, source_target_pairs={{0,64},{64,0},{1,65},{65,1},{2,66},{66,2},{3,67},{67,3},{4,68},{68... | collective-permute-start | bytes 4718600 | tf_op jit(solution)/shard_map/ppermute | solution.py:248
  11.9 1.2 copy-start.7
  11.9 21.9 %copy-start.10 = (bf16[2,256,512]{2,1,0:T(8,128)(2,1)}, bf16[2,256,512]{2,1,0:T(8,128)(2,1)S(1)}, u32[]{:S(2)}) copy-start(bf16[2,256,512]{2,1,0:T(8,128)(2,1)S(1)} %get-tuple-element.73) | copy-start | bytes 1572868
  13.1 21.0 %copy-start.23 = (bf16[4,256,512]{2,1,0:T(8,128)(2,1)S(1)}, bf16[4,256,512]{2,1,0:T(8,128)(2,1)}, u32[]{:S(2)}) copy-start(bf16[4,256,512]{2,1,0:T(8,128)(2,1)} %param.13) | copy-start | bytes 3145732
  33.7 1.0 copy-start.24
  34.7 1.4 copy-start.20
  37.8 2.8 %copy-start = (bf16[512,1536]{1,0:T(8,128)(2,1)}, bf16[512,1536]{1,0:T(8,128)(2,1)S(1)}, u32[]{:S(2)}) copy-start(bf16[512,1536]{1,0:T(8,128)(2,1)S(1)} %get-tuple-element.71) | copy-start | bytes 4718596
  37.8 45.2 %copy-start.3 = (bf16[512,1536]{1,0:T(8,128)(2,1)}, bf16[512,1536]{1,0:T(8,128)(2,1)S(1)}, u32[]{:S(2)}) copy-start(bf16[512,1536]{1,0:T(8,128)(2,1)S(1)} %get-tuple-element.70) | copy-start | bytes 4718596
  38.4 1.3 copy-start.12
  39.7 0.9 copy-start.13
  40.6 0.9 copy-start.14
  41.5 0.9 copy-start.15
  41.5 1.4 slice-start
  82.9 1.3 copy-start.16
  84.9 2.8 %slice-start.1 = ((bf16[256,1536]{1,0:T(8,128)(2,1)}), bf16[256,1024]{1,0:T(8,128)(2,1)S(1)}, s32[]{:S(2)}) async-start(bf16[256,1536]{1,0:T(8,128)(2,1)} %copy-done.13), calls=%async_computation.1 | async-start | bytes 1048576 | tf_op jit(solution)/shard_map/slice | solution.py:270
  120.7 1.8 copy-start.4
  120.9 2.9 %copy-start.17 = (bf16[512,1024]{1,0:T(8,128)(2,1)}, bf16[512,1024]{1,0:T(8,128)(2,1)S(1)}, u32[]{:S(2)}) copy-start(bf16[512,1024]{1,0:T(8,128)(2,1)S(1)} %maximum_convert_fusion.1) | copy-start | bytes 3145732
  125.7 2.0 copy-start.5
  125.7 2.0 copy-start.8
  125.7 2.0 slice-start.4
  127.8 1.0 copy-start.22
  127.8 1.2 slice-start.3
  130.8 1.3 copy-start.25
  163.5 1.4 copy-start.1
  164.9 1.0 copy-start.18
  167.8 2.0 slice-start.5
  169.5 1.4 copy-start.6
  169.5 1.5 copy-start.9
  171.0 1.0 slice-start.2
  173.9 1.3 copy-start.26
  205.3 1.4 copy-start.2
  206.7 1.0 copy-start.19
  208.9 18.2 %slice-start.7 = ((bf16[512,1024]{1,0:T(8,128)(2,1)}), bf16[256,1024]{1,0:T(8,128)(2,1)S(1)}, s32[]{:S(2)}) async-start(bf16[512,1024]{1,0:T(8,128)(2,1)} %copy-done.19), calls=%async_computation.7 | async-start | bytes 1048576 | tf_op jit(solution)/shard_map/slice | solution.py:299
  227.1 1.0 copy-start.11
  227.1 1.2 slice-start.6
  230.0 5.2 %collective-permute-start.5 = (bf16[2,256,512]{2,1,0:T(8,128)(2,1)S(1)}, bf16[2,256,512]{2,1,0:T(8,128)(2,1)S(1)}, u32[]{:S(2)}, u32[]{:S(2)}) collective-permute-start(bf16[2,256,512]{2,1,0:T(8,128)(2,1)S(1)} %pad_maximum_fusion.6), channel_id=1, source_target_pairs={{0,64},{64,0},{1,65},{65,1},{2,66},{66,2},{3,67},{67,3},{4,68},{68... | collective-permute-start | bytes 1572872 | tf_op jit(solution)/shard_map/ppermute | solution.py:248

commit v2 on v1

--- a/solution.py
+++ b/solution.py
@@ -80,10 +80,13 @@
         return carry
 
     heads = q_ref.shape[1] // HD
-    split = min(heads, 2 * per_group)
-    lax.fori_loop(0, split, head, 0, unroll=2)
-    after_first()
-    lax.fori_loop(split, heads, head, 0, unroll=2)
+    if after_first is None:
+        lax.fori_loop(0, heads, head, 0, unroll=4)
+    else:
+        split = min(heads, 2 * per_group)
+        lax.fori_loop(0, split, head, 0, unroll=2)
+        after_first()
+        lax.fori_loop(split, heads, head, 0, unroll=2)
 
 
 def exchange_start(spreads, payload_refs, out_refs, send_sems, recv_sems):
@@ -199,7 +202,7 @@
     send_sems, recv_sems = refs[inputs + 2 * count + outputs :]
     relay, finish = exchange_start(spreads, payload_refs, out_refs, send_sems, recv_sems)
     if with_attention:
-        attention_body(*attention_in, *attention_out, relay)
+        attention_body(*attention_in, *attention_out, relay if not any(spreads) else None)
     else:
         relay()
     finish()

time: 240 us -> 237 us (0.988)
  Pallas kernels: 168 us -> 164 us
    pallas_call x6, Pallas kernels: 168 us -> 164 us  [fused_step(): pl.pallas_call(functools.partial(fused_kernel, tuple(spreads), bool(atten...]
  transfers between devices with their start and end apart: 6 -> 6, of which waited for: 1 -> 1; matrix products, arithmetic and copies ran while one was open for 5% -> 5% of each run, Pallas kernels for 8% -> 9%
where the time goes in v2:
time: 237 us; the launch traced here: 233 us
  Pallas kernels  164 us (69%)
  local copies, waits for them, and re-layouts  24.5 us (10%)
  other arithmetic  18.4 us (8%)
  matrix products  17.7 us (7%)
  starting transfers between devices  5.41 us (2%)
    pallas_call x6, Pallas kernels, fused_step(): pl.pallas_call(functools.partial(fused_kernel, tuple(spreads), bool(atten...  164 us
    unnamed x54, local copies, waits for them, and re-layouts  10.8 us
    dot_general x4, matrix products, attach(): jnp.dot(fetched, weight_in[:, model_width:], preferred_element_type=jnp.f...  5.69 us
    ppermute x6, starting transfers between devices, swap_cores(): return lax.ppermute(value, 'pipe', [(0, 1), (1, 0)])  5.41 us
    eq x8, other arithmetic, outgoing(): slots == unit['window_at'][entry]  5.06 us
  transfers between devices with their start and end apart: 6, of which 1 were waited for; matrix products, arithmetic and copies ran while one was open for 5% of the time, Pallas kernels for 9%

profile of v2, /device:TPU:15, one launch (start us, length us, event | category | flops | bytes accessed | tf_op | source)
XLA Modules:
  0.0 232.7 jit_solution(2798169987678828855)
XLA Ops:
  0.0 0.8 reshape_squeeze.9
  1.0 0.7 collective-permute-start.3
  1.8 1.1 dynamic-slice_bitcast_fusion
  2.9 0.5 collective-permute-start
  4.0 0.7 fusion.137
  4.7 0.7 fusion.135
  5.4 0.7 fusion.103
  6.1 0.6 fusion.102
  6.8 0.6 fusion.104
  7.6 0.6 fusion.105
  8.3 0.6 fusion.99
  9.0 0.6 fusion.98
  9.7 0.7 fusion.100
  10.4 0.6 fusion.101
  11.1 0.7 broadcast_select_fusion.13
  13.1 20.0 %shard_map.64 = bf16[4,256,512]{2,1,0:T(8,128)(2,1)S(1)} custom-call(bf16[256,512]{1,0:T(8,128)(2,1)S(1)} %get-tuple-element.87.refs_0_), custom_call_target="tpu_custom_call" | custom-call | bytes 1048577 | tf_op jit(solution)/shard_map/pallas_call | solution.py:229
  33.1 0.6 gather_fusion
  34.1 0.7 copy-done.24
  35.5 0.7 copy-done.20
  36.2 1.6 broadcast_select_fusion.1
  37.8 0.6 convolution_convert_fusion.3
  38.4 0.6 convolution_convert_fusion.2
  39.0 0.7 copy-done.12
  39.7 0.6 convolution_convert_fusion
  40.6 0.6 convolution_convert_fusion.1
  41.5 0.9 copy-done.15
  43.0 39.8 %shard_map.65 = (f32[256,512]{1,0:T(8,128)S(1)}, f32[512,512]{1,0:T(8,128)S(1)}, f32[512,512]{1,0:T(8,128)S(1)}, bf16[4,256,512]{2,1,0:T(8,128)(2,1)S(1)}, bf16[...) custom-call(bf16[256,512]{1,0:T(8,128)(2,1)S(1)} %slice.241.refs_0_, ...), custom_call_target="tpu_custom_call" | custom-call | flops 5368709120 | bytes 3145729 | tf_op jit(solution)/shard_map/pallas_call | solution.py:229
  83.0 1.3 fusion.32
  84.2 0.6 gather_fusion.1
  84.9 1.7 convolution_convert_fusion.6
  86.6 1.1 fusion.134
  88.3 1.2 fusion.7.refs_4_
  89.6 29.9 %shard_map.66 = (f32[256,512]{1,0:T(8,128)S(1)}, f32[512,512]{1,0:T(8,128)S(1)}, f32[512,512]{1,0:T(8,128)S(1)}, bf16[4,256,512]{2,1,0:T(8,128)(2,1)S(1)}) custom-call(bf16[256,512]{1,0:T(8,128)(2,1)S(1)} %slice.250.refs_0_, bf16[512,512]{1,0:T(8,128)(2,1)S(1)} %get-tuple-element.79.refs_1_, bf16[512,512]{1,0:T(8,128)(2,1)S(1)} %get-tuple-element.78.refs_2_, ...), custom_call_target="tpu_custom_call" | custom-call | flops 5368709120 | bytes 4194305 | tf_op jit(solution)/shard_map/pallas_call | solution.py:229
  119.7 1.6 copy-done.4
  121.3 1.3 fusion.30
  122.6 1.8 gather_fusion.2
  124.5 1.8 convolution_convert_fusion.5
  126.6 0.7 fusion.124
  127.8 1.2 fusion.47
  129.6 1.2 fusion.5.refs_4_
  130.8 1.4 convolution_convert_fusion.9.refs_3_
  132.2 28.9 %shard_map.67 = (f32[256,512]{1,0:T(8,128)S(1)}, f32[512,512]{1,0:T(8,128)S(1)}, f32[512,512]{1,0:T(8,128)S(1)}, bf16[4,256,512]{2,1,0:T(8,128)(2,1)S(1)}) custom-call(bf16[256,512]{1,0:T(8,128)(2,1)S(1)} %slice.257.refs_0_, bf16[512,512]{1,0:T(8,128)(2,1)S(1)} %get-tuple-element.81.refs_1_, bf16[512,512]{1,0:T(8,128)(2,1)S(1)} %get-tuple-element.80.refs_2_, ...), custom_call_target="tpu_custom_call" | custom-call | flops 5368709120 | bytes 4194305 | tf_op jit(solution)/shard_map/pallas_call | solution.py:229
  161.2 1.3 copy-done.1
  162.5 0.5 fusion.26
  163.0 0.5 copy-done.18
  163.5 1.8 gather_fusion.3
  165.4 1.7 convolution_convert_fusion.4
  167.3 1.2 copy-done.6
  168.6 0.7 fusion.123
  169.7 1.2 fusion.60
  171.5 1.2 fusion.3.refs_4_
  172.7 1.4 convolution_convert_fusion.8.refs_3_
  174.1 27.6 %shard_map.68 = (f32[256,512]{1,0:T(8,128)S(1)}, f32[512,512]{1,0:T(8,128)S(1)}, f32[512,512]{1,0:T(8,128)S(1)}, bf16[4,256,512]{2,1,0:T(8,128)(2,1)S(1)}) custom-call(bf16[256,512]{1,0:T(8,128)(2,1)S(1)} %slice.266.refs_0_, bf16[512,512]{1,0:T(8,128)(2,1)S(1)} %get-tuple-element.77.refs_1_, bf16[512,512]{1,0:T(8,128)(2,1)S(1)} %get-tuple-element.76.refs_2_, ...), custom_call_target="tpu_custom_call" | custom-call | flops 5368709120 | bytes 4194305 | tf_op jit(solution)/shard_map/pallas_call | solution.py:229
  201.8 1.3 copy-done.2
  203.1 0.5 fusion.24
  203.5 0.5 copy-done.19
  204.8 0.5 fusion.1.refs_0_
  205.3 18.0 %shard_map.69 = bf16[4,256,512]{2,1,0:T(8,128)(2,1)S(1)} custom-call(bf16[4,256,512]{2,1,0:T(8,128)(2,1)S(1)} %fusion.1.refs_0_), custom_call_target="tpu_custom_call" | custom-call | bytes 4194305 | tf_op jit(solution)/shard_map/pallas_call | solution.py:229
  223.5 0.6 fusion.8
  224.7 0.8 fusion.122
  225.5 0.7 select_bitcast_fusion.5
  226.3 3.6 %collective-permute-start.5 = (bf16[2,256,512]{2,1,0:T(8,128)(2,1)S(1)}, bf16[2,256,512]{2,1,0:T(8,128)(2,1)S(1)}, u32[]{:S(2)}, u32[]{:S(2)}) collective-permute-start(bf16[2,256,512]{2,1,0:T(8,128)(2,1)S(1)} %pad_maximum_fusion.6), channel_id=1, source_target_pairs={{0,64},{64,0},{1,65},{65,1},{2,66},{66,2},{3,67},{67,3},{4,68},{68... | collective-permute-start | bytes 1572872 | tf_op jit(solution)/shard_map/ppermute | solution.py:251
  230.0 1.5 collective-permute-done.5
  231.7 1.0 copy.15
  (153 shorter events, 10.6 us)
Async XLA Ops:
  0.0 11.8 %copy-start.21 = (bf16[1,4,256,512]{3,2,1,0:T(8,128)(2,1)S(1)}, bf16[1,4,256,512]{3,2,1,0:T(8,128)(2,1)}, u32[]{:S(2)}) copy-start(bf16[1,4,256,512]{3,2,1,0:T(8,128)(2,1)} %param.8) | copy-start | bytes 3145732
  1.0 3.0 %collective-permute-start.3 = (s32[2,2]{1,0:T(2,128)S(1)}, s32[2,2]{1,0:T(2,128)S(1)}, u32[]{:S(2)}, u32[]{:S(2)}) collective-permute-start(s32[2,2]{1,0:T(2,128)S(1)} %bitcast.354), channel_id=1, source_target_pairs={{0,64},{64,0},{1,65},{65,1},{2,66},{66,2},{3,67},{67,3},{4,68},{68... | collective-permute-start | bytes 56 | tf_op jit(solution)/shard_map/ppermute | solution.py:251
  1.7 9.4 %collective-permute-start.1 = (f32[512]{0:T(512)}, f32[512]{0:T(512)S(1)}, u32[]{:S(2)}, u32[]{:S(2)}) collective-permute-start(f32[512]{0:T(512)} %bitcast.352), channel_id=1, source_target_pairs={{0,64},{64,0},{1,65},{65,1},{2,66},{66,2},{3,67},{67,3},{4,68},{68... | collective-permute-start | bytes 6152 | tf_op jit(solution)/shard_map/ppermute | solution.py:251
  2.9 9.0 %collective-permute-start = (bf16[2,256,512]{2,1,0:T(8,128)(2,1)S(1)}, bf16[2,256,512]{2,1,0:T(8,128)(2,1)S(1)}, u32[]{:S(2)}, u32[]{:S(2)}) collective-permute-start(bf16[2,256,512]{2,1,0:T(8,128)(2,1)S(1)} %dynamic-slice_bitcast_fusion), channel_id=1, source_target_pairs={{0,64},{64,0},{1,65},{65,1},{2,66},{66,2},{3,67},{67,3},{4,68},{68... | collective-permute-start | bytes 1572872 | tf_op jit(solution)/shard_map/ppermute | solution.py:251
  3.4 30.7 %collective-permute-start.4 = (bf16[512,512]{1,0:T(8,128)(2,1)}, bf16[512,512]{1,0:T(8,128)(2,1)}, u32[]{:S(2)}, u32[]{:S(2)}) collective-permute-start(bf16[512,512]{1,0:T(8,128)(2,1)} %bitcast.355), channel_id=1, source_target_pairs={{0,64},{64,0},{1,65},{65,1},{2,66},{66,2},{3,67},{67,3},{4,68},{68... | collective-permute-start | bytes 1572872 | tf_op jit(solution)/shard_map/ppermute | solution.py:251
  3.5 32.0 %collective-permute-start.2 = (bf16[512,1536]{1,0:T(8,128)(2,1)}, bf16[512,1536]{1,0:T(8,128)(2,1)}, u32[]{:S(2)}, u32[]{:S(2)}) collective-permute-start(bf16[512,1536]{1,0:T(8,128)(2,1)} %bitcast.339), channel_id=1, source_target_pairs={{0,64},{64,0},{1,65},{65,1},{2,66},{66,2},{3,67},{67,3},{4,68},{68... | collective-permute-start | bytes 4718600 | tf_op jit(solution)/shard_map/ppermute | solution.py:251
  11.9 1.2 copy-start.7
  11.9 21.9 %copy-start.10 = (bf16[2,256,512]{2,1,0:T(8,128)(2,1)}, bf16[2,256,512]{2,1,0:T(8,128)(2,1)S(1)}, u32[]{:S(2)}) copy-start(bf16[2,256,512]{2,1,0:T(8,128)(2,1)S(1)} %get-tuple-element.73) | copy-start | bytes 1572868
  13.1 21.0 %copy-start.23 = (bf16[4,256,512]{2,1,0:T(8,128)(2,1)S(1)}, bf16[4,256,512]{2,1,0:T(8,128)(2,1)}, u32[]{:S(2)}) copy-start(bf16[4,256,512]{2,1,0:T(8,128)(2,1)} %param.13) | copy-start | bytes 3145732
  33.7 1.0 copy-start.24
  34.7 1.4 copy-start.20
  37.8 2.8 %copy-start = (bf16[512,1536]{1,0:T(8,128)(2,1)}, bf16[512,1536]{1,0:T(8,128)(2,1)S(1)}, u32[]{:S(2)}) copy-start(bf16[512,1536]{1,0:T(8,128)(2,1)S(1)} %get-tuple-element.71) | copy-start | bytes 4718596
  37.8 45.2 %copy-start.3 = (bf16[512,1536]{1,0:T(8,128)(2,1)}, bf16[512,1536]{1,0:T(8,128)(2,1)S(1)}, u32[]{:S(2)}) copy-start(bf16[512,1536]{1,0:T(8,128)(2,1)S(1)} %get-tuple-element.70) | copy-start | bytes 4718596
  38.4 1.3 copy-start.12
  39.7 0.9 copy-start.13
  40.6 0.9 copy-start.14
  41.5 0.9 copy-start.15
  41.5 1.4 slice-start
  82.9 1.3 copy-start.16
  84.9 2.8 %slice-start.1 = ((bf16[256,1536]{1,0:T(8,128)(2,1)}), bf16[256,1024]{1,0:T(8,128)(2,1)S(1)}, s32[]{:S(2)}) async-start(bf16[256,1536]{1,0:T(8,128)(2,1)} %copy-done.13), calls=%async_computation.1 | async-start | bytes 1048576 | tf_op jit(solution)/shard_map/slice | solution.py:273
  119.5 1.8 copy-start.4
  119.7 2.9 %copy-start.17 = (bf16[512,1024]{1,0:T(8,128)(2,1)}, bf16[512,1024]{1,0:T(8,128)(2,1)S(1)}, u32[]{:S(2)}) copy-start(bf16[512,1024]{1,0:T(8,128)(2,1)S(1)} %maximum_convert_fusion.1) | copy-start | bytes 3145732
  124.5 2.0 copy-start.5
  124.5 2.0 copy-start.8
  124.5 2.0 slice-start.4
  126.5 1.0 copy-start.22
  126.5 1.2 slice-start.3
  129.5 1.3 copy-start.25
  161.1 1.4 copy-start.1
  162.5 1.0 copy-start.18
  165.3 2.0 slice-start.5
  167.1 1.4 copy-start.6
  167.1 1.5 copy-start.9
  168.6 1.0 slice-start.2
  171.5 1.3 copy-start.26
  201.7 1.4 copy-start.2
  203.1 1.0 copy-start.19
  205.3 18.2 %slice-start.7 = ((bf16[512,1024]{1,0:T(8,128)(2,1)}), bf16[256,1024]{1,0:T(8,128)(2,1)S(1)}, s32[]{:S(2)}) async-start(bf16[512,1024]{1,0:T(8,128)(2,1)} %copy-done.19), calls=%async_computation.7 | async-start | bytes 1048576 | tf_op jit(solution)/shard_map/slice | solution.py:302
  223.5 1.0 copy-start.11
  223.5 1.2 slice-start.6
  226.3 5.2 %collective-permute-start.5 = (bf16[2,256,512]{2,1,0:T(8,128)(2,1)S(1)}, bf16[2,256,512]{2,1,0:T(8,128)(2,1)S(1)}, u32[]{:S(2)}, u32[]{:S(2)}) collective-permute-start(bf16[2,256,512]{2,1,0:T(8,128)(2,1)S(1)} %pad_maximum_fusion.6), channel_id=1, source_target_pairs={{0,64},{64,0},{1,65},{65,1},{2,66},{66,2},{3,67},{67,3},{4,68},{68... | collective-permute-start | bytes 1572872 | tf_op jit(solution)/shard_map/ppermute | solution.py:251

commit v3 on v2

--- a/solution.py
+++ b/solution.py
@@ -44,7 +44,7 @@
 OFFSETS = [shift_by for shift_by in range(-REACH, REACH + 1) if shift_by != 0]
 
 
-def attention_body(q_ref, k_ref, v_ref, g_ref, dq_ref, dk_ref, dv_ref, after_first):
+def attention_body(q_ref, k_ref, v_ref, g_ref, dq_ref, dk_ref, dv_ref, hooks):
     factor = HD ** (-0.5)
     group = 128
     per_group = group // HD
@@ -80,13 +80,15 @@
         return carry
 
     heads = q_ref.shape[1] // HD
-    if after_first is None:
+    if not hooks:
         lax.fori_loop(0, heads, head, 0, unroll=4)
     else:
-        split = min(heads, 2 * per_group)
-        lax.fori_loop(0, split, head, 0, unroll=2)
-        after_first()
-        lax.fori_loop(split, heads, head, 0, unroll=2)
+        begin = 0
+        for edge in sorted(hooks):
+            lax.fori_loop(begin, edge, head, 0, unroll=2)
+            hooks[edge]()
+            begin = edge
+        lax.fori_loop(begin, heads, head, 0, unroll=2)
 
 
 def exchange_start(spreads, payload_refs, out_refs, send_sems, recv_sems):
@@ -152,14 +154,15 @@
                 )
                 relayed.append((which, shift_by, forward, exists(shift_by) & exists(-shift_by)))
 
-    def relay():
-        for which, shift_by, forward, valid in relayed:
+    def relay(whiches):
+        chosen = [entry for entry in relayed if entry[0] in whiches]
+        for which, shift_by, forward, valid in chosen:
 
             @pl.when(exists(-shift_by))
             def _():
                 arrival(which, slot(-shift_by)).wait_recv()
 
-        for which, shift_by, forward, valid in relayed:
+        for which, shift_by, forward, valid in chosen:
 
             @pl.when(valid)
             def _():
@@ -202,9 +205,15 @@
     send_sems, recv_sems = refs[inputs + 2 * count + outputs :]
     relay, finish = exchange_start(spreads, payload_refs, out_refs, send_sems, recv_sems)
     if with_attention:
-        attention_body(*attention_in, *attention_out, relay if not any(spreads) else None)
+        hooks = {}
+        if not any(spreads):
+            heads = attention_in[0].shape[1] // HD
+            for which in range(count):
+                edge = (which + 1) * heads // (count + 1)
+                hooks[edge] = functools.partial(relay, [which])
+        attention_body(*attention_in, *attention_out, hooks)
     else:
-        relay()
+        relay(list(range(count)))
     finish()
 
 

time: 237 us -> 236 us (level)
  no operation moved by 1% of the time
where the time goes in v3:
time: 236 us; the launch traced here: 233 us
  Pallas kernels  165 us (70%)
  local copies, waits for them, and re-layouts  24.5 us (10%)
  other arithmetic  18.4 us (8%)
  matrix products  17.7 us (8%)
  starting transfers between devices  4.39 us (2%)
    pallas_call x6, Pallas kernels, fused_step(): pl.pallas_call(functools.partial(fused_kernel, tuple(spreads), bool(atten...  165 us
    unnamed x54, local copies, waits for them, and re-layouts  10.8 us
    dot_general x4, matrix products, attach(): jnp.dot(fetched, weight_in[:, model_width:], preferred_element_type=jnp.f...  5.69 us
    eq x8, other arithmetic, outgoing(): slots == unit['window_at'][entry]  5.06 us
  transfers between devices with their start and end apart: 6, of which 1 were waited for; matrix products, arithmetic and copies ran while one was open for 5% of the time, Pallas kernels for 9%

profile of v3, /device:TPU:15, one launch (start us, length us, event | category | flops | bytes accessed | tf_op | source)
XLA Modules:
  0.0 232.9 jit_solution(12396387746656591018)
XLA Ops:
  0.0 0.8 reshape_squeeze.9
  1.0 0.7 collective-permute-start.3
  1.8 1.1 dynamic-slice_bitcast_fusion
  2.9 0.5 collective-permute-start
  4.0 0.7 fusion.137
  4.7 0.7 fusion.135
  5.4 0.7 fusion.103
  6.1 0.6 fusion.102
  6.8 0.6 fusion.104
  7.6 0.6 fusion.105
  8.3 0.6 fusion.99
  9.0 0.6 fusion.98
  9.7 0.7 fusion.100
  10.4 0.6 fusion.101
  11.1 0.7 broadcast_select_fusion.13
  13.1 20.0 %shard_map.64 = bf16[4,256,512]{2,1,0:T(8,128)(2,1)S(1)} custom-call(bf16[256,512]{1,0:T(8,128)(2,1)S(1)} %get-tuple-element.87.refs_0_), custom_call_target="tpu_custom_call" | custom-call | bytes 1048577 | tf_op jit(solution)/shard_map/pallas_call | solution.py:238
  33.1 0.6 gather_fusion
  34.1 0.7 copy-done.24
  35.5 0.7 copy-done.20
  36.2 1.6 broadcast_select_fusion.1
  37.8 0.6 convolution_convert_fusion.3
  38.4 0.6 convolution_convert_fusion.2
  39.0 0.7 copy-done.12
  39.7 0.6 convolution_convert_fusion
  40.6 0.6 convolution_convert_fusion.1
  41.5 0.9 copy-done.15
  43.0 39.2 %shard_map.65 = (f32[256,512]{1,0:T(8,128)S(1)}, f32[512,512]{1,0:T(8,128)S(1)}, f32[512,512]{1,0:T(8,128)S(1)}, bf16[4,256,512]{2,1,0:T(8,128)(2,1)S(1)}, bf16[...) custom-call(bf16[256,512]{1,0:T(8,128)(2,1)S(1)} %slice.241.refs_0_, ...), custom_call_target="tpu_custom_call" | custom-call | flops 5368709120 | bytes 3145729 | tf_op jit(solution)/shard_map/pallas_call | solution.py:238
  82.4 1.3 fusion.32
  83.6 0.6 gather_fusion.1
  84.3 1.7 convolution_convert_fusion.6
  86.0 1.1 fusion.134
  87.7 1.2 fusion.7.refs_4_
  89.0 29.9 %shard_map.66 = (f32[256,512]{1,0:T(8,128)S(1)}, f32[512,512]{1,0:T(8,128)S(1)}, f32[512,512]{1,0:T(8,128)S(1)}, bf16[4,256,512]{2,1,0:T(8,128)(2,1)S(1)}) custom-call(bf16[256,512]{1,0:T(8,128)(2,1)S(1)} %slice.250.refs_0_, bf16[512,512]{1,0:T(8,128)(2,1)S(1)} %get-tuple-element.79.refs_1_, bf16[512,512]{1,0:T(8,128)(2,1)S(1)} %get-tuple-element.78.refs_2_, ...), custom_call_target="tpu_custom_call" | custom-call | flops 5368709120 | bytes 4194305 | tf_op jit(solution)/shard_map/pallas_call | solution.py:238
  119.1 1.6 copy-done.4
  120.7 1.3 fusion.30
  122.0 1.8 gather_fusion.2
  123.9 1.8 convolution_convert_fusion.5
  126.0 0.7 fusion.124
  127.2 1.2 fusion.47
  129.0 1.2 fusion.5.refs_4_
  130.2 1.4 convolution_convert_fusion.9.refs_3_
  131.6 29.7 %shard_map.67 = (f32[256,512]{1,0:T(8,128)S(1)}, f32[512,512]{1,0:T(8,128)S(1)}, f32[512,512]{1,0:T(8,128)S(1)}, bf16[4,256,512]{2,1,0:T(8,128)(2,1)S(1)}) custom-call(bf16[256,512]{1,0:T(8,128)(2,1)S(1)} %slice.257.refs_0_, bf16[512,512]{1,0:T(8,128)(2,1)S(1)} %get-tuple-element.81.refs_1_, bf16[512,512]{1,0:T(8,128)(2,1)S(1)} %get-tuple-element.80.refs_2_, ...), custom_call_target="tpu_custom_call" | custom-call | flops 5368709120 | bytes 4194305 | tf_op jit(solution)/shard_map/pallas_call | solution.py:238
  161.5 1.3 copy-done.1
  162.7 0.5 fusion.26
  163.2 0.5 copy-done.18
  163.7 1.8 gather_fusion.3
  165.6 1.7 convolution_convert_fusion.4
  167.5 1.2 copy-done.6
  168.8 0.7 fusion.123
  170.0 1.2 fusion.60
  171.7 1.2 fusion.3.refs_4_
  173.0 1.4 convolution_convert_fusion.8.refs_3_
  174.3 26.7 %shard_map.68 = (f32[256,512]{1,0:T(8,128)S(1)}, f32[512,512]{1,0:T(8,128)S(1)}, f32[512,512]{1,0:T(8,128)S(1)}, bf16[4,256,512]{2,1,0:T(8,128)(2,1)S(1)}) custom-call(bf16[256,512]{1,0:T(8,128)(2,1)S(1)} %slice.266.refs_0_, bf16[512,512]{1,0:T(8,128)(2,1)S(1)} %get-tuple-element.77.refs_1_, bf16[512,512]{1,0:T(8,128)(2,1)S(1)} %get-tuple-element.76.refs_2_, ...), custom_call_target="tpu_custom_call" | custom-call | flops 5368709120 | bytes 4194305 | tf_op jit(solution)/shard_map/pallas_call | solution.py:238
  201.2 1.3 copy-done.2
  202.5 0.5 fusion.24
  202.9 0.5 copy-done.19
  204.2 0.5 fusion.1.refs_0_
  204.7 19.8 %shard_map.69 = bf16[4,256,512]{2,1,0:T(8,128)(2,1)S(1)} custom-call(bf16[4,256,512]{2,1,0:T(8,128)(2,1)S(1)} %fusion.1.refs_0_), custom_call_target="tpu_custom_call" | custom-call | bytes 4194305 | tf_op jit(solution)/shard_map/pallas_call | solution.py:238
  224.7 0.6 fusion.8
  225.9 0.8 fusion.122
  226.7 0.7 select_bitcast_fusion.5
  227.5 2.6 %collective-permute-start.5 = (bf16[2,256,512]{2,1,0:T(8,128)(2,1)S(1)}, bf16[2,256,512]{2,1,0:T(8,128)(2,1)S(1)}, u32[]{:S(2)}, u32[]{:S(2)}) collective-permute-start(bf16[2,256,512]{2,1,0:T(8,128)(2,1)S(1)} %pad_maximum_fusion.6), channel_id=1, source_target_pairs={{0,64},{64,0},{1,65},{65,1},{2,66},{66,2},{3,67},{67,3},{4,68},{68... | collective-permute-start | bytes 1572872 | tf_op jit(solution)/shard_map/ppermute | solution.py:260
  230.2 1.5 collective-permute-done.5
  231.9 1.0 copy.15
  (153 shorter events, 10.6 us)
Async XLA Ops:
  0.0 11.8 %copy-start.21 = (bf16[1,4,256,512]{3,2,1,0:T(8,128)(2,1)S(1)}, bf16[1,4,256,512]{3,2,1,0:T(8,128)(2,1)}, u32[]{:S(2)}) copy-start(bf16[1,4,256,512]{3,2,1,0:T(8,128)(2,1)} %param.8) | copy-start | bytes 3145732
  1.0 3.0 %collective-permute-start.3 = (s32[2,2]{1,0:T(2,128)S(1)}, s32[2,2]{1,0:T(2,128)S(1)}, u32[]{:S(2)}, u32[]{:S(2)}) collective-permute-start(s32[2,2]{1,0:T(2,128)S(1)} %bitcast.354), channel_id=1, source_target_pairs={{0,64},{64,0},{1,65},{65,1},{2,66},{66,2},{3,67},{67,3},{4,68},{68... | collective-permute-start | bytes 56 | tf_op jit(solution)/shard_map/ppermute | solution.py:260
  1.7 9.4 %collective-permute-start.1 = (f32[512]{0:T(512)}, f32[512]{0:T(512)S(1)}, u32[]{:S(2)}, u32[]{:S(2)}) collective-permute-start(f32[512]{0:T(512)} %bitcast.352), channel_id=1, source_target_pairs={{0,64},{64,0},{1,65},{65,1},{2,66},{66,2},{3,67},{67,3},{4,68},{68... | collective-permute-start | bytes 6152 | tf_op jit(solution)/shard_map/ppermute | solution.py:260
  2.9 9.0 %collective-permute-start = (bf16[2,256,512]{2,1,0:T(8,128)(2,1)S(1)}, bf16[2,256,512]{2,1,0:T(8,128)(2,1)S(1)}, u32[]{:S(2)}, u32[]{:S(2)}) collective-permute-start(bf16[2,256,512]{2,1,0:T(8,128)(2,1)S(1)} %dynamic-slice_bitcast_fusion), channel_id=1, source_target_pairs={{0,64},{64,0},{1,65},{65,1},{2,66},{66,2},{3,67},{67,3},{4,68},{68... | collective-permute-start | bytes 1572872 | tf_op jit(solution)/shard_map/ppermute | solution.py:260
  3.4 30.7 %collective-permute-start.4 = (bf16[512,512]{1,0:T(8,128)(2,1)}, bf16[512,512]{1,0:T(8,128)(2,1)}, u32[]{:S(2)}, u32[]{:S(2)}) collective-permute-start(bf16[512,512]{1,0:T(8,128)(2,1)} %bitcast.355), channel_id=1, source_target_pairs={{0,64},{64,0},{1,65},{65,1},{2,66},{66,2},{3,67},{67,3},{4,68},{68... | collective-permute-start | bytes 1572872 | tf_op jit(solution)/shard_map/ppermute | solution.py:260
  3.5 32.0 %collective-permute-start.2 = (bf16[512,1536]{1,0:T(8,128)(2,1)}, bf16[512,1536]{1,0:T(8,128)(2,1)}, u32[]{:S(2)}, u32[]{:S(2)}) collective-permute-start(bf16[512,1536]{1,0:T(8,128)(2,1)} %bitcast.339), channel_id=1, source_target_pairs={{0,64},{64,0},{1,65},{65,1},{2,66},{66,2},{3,67},{67,3},{4,68},{68... | collective-permute-start | bytes 4718600 | tf_op jit(solution)/shard_map/ppermute | solution.py:260
  11.9 1.2 copy-start.7
  11.9 21.9 %copy-start.10 = (bf16[2,256,512]{2,1,0:T(8,128)(2,1)}, bf16[2,256,512]{2,1,0:T(8,128)(2,1)S(1)}, u32[]{:S(2)}) copy-start(bf16[2,256,512]{2,1,0:T(8,128)(2,1)S(1)} %get-tuple-element.73) | copy-start | bytes 1572868
  13.1 21.0 %copy-start.23 = (bf16[4,256,512]{2,1,0:T(8,128)(2,1)S(1)}, bf16[4,256,512]{2,1,0:T(8,128)(2,1)}, u32[]{:S(2)}) copy-start(bf16[4,256,512]{2,1,0:T(8,128)(2,1)} %param.13) | copy-start | bytes 3145732
  33.7 1.0 copy-start.24
  34.7 1.4 copy-start.20
  37.8 2.8 %copy-start = (bf16[512,1536]{1,0:T(8,128)(2,1)}, bf16[512,1536]{1,0:T(8,128)(2,1)S(1)}, u32[]{:S(2)}) copy-start(bf16[512,1536]{1,0:T(8,128)(2,1)S(1)} %get-tuple-element.71) | copy-start | bytes 4718596
  37.8 44.6 %copy-start.3 = (bf16[512,1536]{1,0:T(8,128)(2,1)}, bf16[512,1536]{1,0:T(8,128)(2,1)S(1)}, u32[]{:S(2)}) copy-start(bf16[512,1536]{1,0:T(8,128)(2,1)S(1)} %get-tuple-element.70) | copy-start | bytes 4718596
  38.4 1.3 copy-start.12
  39.7 0.9 copy-start.13
  40.6 0.9 copy-start.14
  41.5 0.9 copy-start.15
  41.5 1.4 slice-start
  82.4 1.3 copy-start.16
  84.3 2.8 %slice-start.1 = ((bf16[256,1536]{1,0:T(8,128)(2,1)}), bf16[256,1024]{1,0:T(8,128)(2,1)S(1)}, s32[]{:S(2)}) async-start(bf16[256,1536]{1,0:T(8,128)(2,1)} %copy-done.13), calls=%async_computation.1 | async-start | bytes 1048576 | tf_op jit(solution)/shard_map/slice | solution.py:282
  118.9 1.8 copy-start.4
  119.1 2.9 %copy-start.17 = (bf16[512,1024]{1,0:T(8,128)(2,1)}, bf16[512,1024]{1,0:T(8,128)(2,1)S(1)}, u32[]{:S(2)}) copy-start(bf16[512,1024]{1,0:T(8,128)(2,1)S(1)} %maximum_convert_fusion.1) | copy-start | bytes 3145732
  123.9 2.0 copy-start.5
  123.9 2.0 copy-start.8
  123.9 2.0 slice-start.4
  125.9 1.0 copy-start.22
  125.9 1.2 slice-start.3
  128.9 1.3 copy-start.25
  161.3 1.4 copy-start.1
  162.7 1.0 copy-start.18
  165.6 2.0 slice-start.5
  167.3 1.4 copy-start.6
  167.3 1.5 copy-start.9
  168.8 1.0 slice-start.2
  171.7 1.3 copy-start.26
  201.1 1.4 copy-start.2
  202.5 1.0 copy-start.19
  204.7 20.0 %slice-start.7 = ((bf16[512,1024]{1,0:T(8,128)(2,1)}), bf16[256,1024]{1,0:T(8,128)(2,1)S(1)}, s32[]{:S(2)}) async-start(bf16[512,1024]{1,0:T(8,128)(2,1)} %copy-done.19), calls=%async_computation.7 | async-start | bytes 1048576 | tf_op jit(solution)/shard_map/slice | solution.py:311
  224.7 1.0 copy-start.11
  224.7 1.2 slice-start.6
  227.5 4.2 %collective-permute-start.5 = (bf16[2,256,512]{2,1,0:T(8,128)(2,1)S(1)}, bf16[2,256,512]{2,1,0:T(8,128)(2,1)S(1)}, u32[]{:S(2)}, u32[]{:S(2)}) collective-permute-start(bf16[2,256,512]{2,1,0:T(8,128)(2,1)S(1)} %pad_maximum_fusion.6), channel_id=1, source_target_pairs={{0,64},{64,0},{1,65},{65,1},{2,66},{66,2},{3,67},{67,3},{4,68},{68... | collective-permute-start | bytes 1572872 | tf_op jit(solution)/shard_map/ppermute | solution.py:260

commit v4 on v3

--- a/solution.py
+++ b/solution.py
@@ -194,16 +194,35 @@
     return relay, finish
 
 
-def fused_kernel(spreads, with_attention, *refs):
+def fused_kernel(spreads, with_attention, projection, *refs):
     count = len(spreads)
     inputs = 4 if with_attention else 0
     outputs = 3 if with_attention else 0
-    attention_in = refs[:inputs]
-    payload_refs = refs[inputs : inputs + count]
-    attention_out = refs[inputs + count : inputs + count + outputs]
-    out_refs = refs[inputs + count + outputs : inputs + 2 * count + outputs]
-    send_sems, recv_sems = refs[inputs + 2 * count + outputs :]
+    extra_in = len(projection) + (max(projection) + 1 if projection else 0)
+    extra_out = 1 if projection else 0
+    position = 0
+
+    def take(number):
+        nonlocal position
+        taken = refs[position : position + number]
+        position += number
+        return taken
+
+    attention_in = take(inputs)
+    payload_refs = take(count)
+    project_in = take(extra_in)
+    attention_out = take(outputs)
+    out_refs = take(count)
+    project_out = take(extra_out)
+    send_sems, recv_sems = take(2)
     relay, finish = exchange_start(spreads, payload_refs, out_refs, send_sems, recv_sems)
+    if projection:
+        rows_refs = project_in[: len(projection)]
+        weight_refs = project_in[len(projection) :]
+        for unit, chosen in enumerate(projection):
+            project_out[0][unit] = jnp.dot(
+                rows_refs[unit][...], weight_refs[chosen][...], preferred_element_type=jnp.float32
+            ).astype(project_out[0].dtype)
     if with_attention:
         hooks = {}
         if not any(spreads):
@@ -217,7 +236,7 @@
     finish()
 
 
-def fused_step(attention_args, payloads, spreads, collective_id):
+def fused_step(attention_args, payloads, spreads, collective_id, projection=None):
     vmem = pl.BlockSpec(memory_space=pltpu.VMEM)
     out_shapes = []
     flops = 0
@@ -235,10 +254,21 @@
         shape = payload.shape[1:] if spread else payload.shape
         out_shapes.append(jax.ShapeDtypeStruct((len(OFFSETS),) + shape, payload.dtype))
     moved = sum(len(OFFSETS) * x.size * x.dtype.itemsize for x in payloads)
+    project_args = []
+    chosen = ()
+    if projection is not None:
+        rows_list, weights, chosen = projection
+        chosen = tuple(chosen)
+        project_args = list(rows_list) + list(weights)
+        rows, width = rows_list[0].shape
+        out_shapes.append(
+            jax.ShapeDtypeStruct((len(rows_list), rows, weights[0].shape[1]), jnp.bfloat16)
+        )
+        flops += 2 * len(rows_list) * rows * width * weights[0].shape[1]
     outs = pl.pallas_call(
-        functools.partial(fused_kernel, tuple(spreads), bool(attention_args)),
+        functools.partial(fused_kernel, tuple(spreads), bool(attention_args), chosen),
         out_shape=out_shapes,
-        in_specs=[vmem] * (len(attention_args) + len(payloads)),
+        in_specs=[vmem] * (len(attention_args) + len(payloads) + len(project_args)),
         out_specs=[vmem] * len(out_shapes),
         scratch_shapes=[
             pltpu.SemaphoreType.DMA((len(payloads), len(OFFSETS))),
@@ -252,7 +282,7 @@
         cost_estimate=pl.CostEstimate(
             flops=flops, transcendentals=flops // 160, bytes_accessed=moved + 1
         ),
-    )(*attention_args, *payloads)
+    )(*attention_args, *payloads, *project_args)
     return list(outs)
 
 
@@ -268,7 +298,6 @@
     points, model_width = rows.shape
     block_count = points // BLK
     scaled, inverse, normed = normalize(rows, gain_row)
-    projected = jnp.dot(normed, weight_in, preferred_element_type=jnp.float32).astype(jnp.bfloat16)
     owners = lists // block_count
     within = lists % block_count
     distance = owners - myself
@@ -278,14 +307,12 @@
         scaled=scaled,
         inverse=inverse,
         normed=normed,
-        queries=projected[:, :model_width],
-        own_pairs=projected[:, model_width:],
         window_at=window_at,
     )
 
 
 def attach(unit, received, weight_in):
-    points, model_width = unit["queries"].shape
+    points, model_width = unit["normed"].shape
     received = received.reshape(len(OFFSETS) * (points // BLK), BLK, model_width)
     fetched = jnp.take(received, unit["window_at"], axis=0).reshape(-1, model_width)
     fetched_pairs = jnp.dot(
@@ -364,7 +391,20 @@
     ]
     results = {}
     ids = iter(range(len(order) + 2))
-    (first_received,) = fused_step((), [units[0]["normed"]], [False], next(ids))
+    first_received, projected = fused_step(
+        (),
+        [units[0]["normed"]],
+        [False],
+        next(ids),
+        projection=(
+            [unit["normed"] for unit in units],
+            [params[section][2] for section in range(sections)],
+            [section for section, _ in order],
+        ),
+    )
+    for unit, rows in zip(units, projected):
+        unit["queries"] = rows[:, :model_width]
+        unit["own_pairs"] = rows[:, model_width:]
     attach(units[0], first_received, params[order[0][0]][2])
     pending = None
     for step, (section, j) in enumerate(order):

time: 236 us -> 246 us (1.042)
  other arithmetic: 18.4 us -> 24.4 us
  local copies, waits for them, and re-layouts: 24.5 us -> 30.5 us
  matrix products: 17.7 us -> 12.1 us
  Pallas kernels: 165 us -> 168 us
    unnamed x54 -> x100, local copies, waits for them, and re-layouts: 10.8 us -> 4.82 us
    gather x4, local copies, waits for them, and re-layouts: 4.7 us -> 10 us  [attach(): jnp.take(received, unit['window_at'], axis=0).reshape(-1, model_width)]
    slice x12 -> x8, local copies, waits for them, and re-layouts: 0.45 us -> 5.65 us  [the longest x4 3.48 us: shards(): unit['own_pairs'] = rows[:, model_width:]]
    select_n x6, other arithmetic: 0.39 us -> 4.59 us  [attach(): jnp.take(received, unit['window_at'], axis=0).reshape(-1, model_width)]
    dot_general x4, matrix products: 5.69 us -> 1.73 us  [attach(): jnp.dot(fetched, weight_in[:, model_width:], preferred_element_type=jnp.f...]
    pallas_call x6, Pallas kernels: 165 us -> 168 us  [fused_step(): pl.pallas_call(functools.partial(fused_kernel, tuple(spreads), bool(atten...]
  transfers between devices with their start and end apart: 6 -> 6, of which waited for: 1 -> 1; matrix products, arithmetic and copies ran while one was open for 5% -> 6% of each run, Pallas kernels for 9% -> 0%
where the time goes in v4:
time: 246 us; the launch traced here: 242 us
  Pallas kernels  168 us (68%)
  local copies, waits for them, and re-layouts  30.5 us (12%)
  other arithmetic  24.4 us (10%)
  matrix products  12.1 us (5%)
  starting transfers between devices  4.64 us (2%)
    pallas_call x6, Pallas kernels, fused_step(): pl.pallas_call(functools.partial(fused_kernel, tuple(spreads), bool(atten...  168 us
    gather x4, local copies, waits for them, and re-layouts, attach(): jnp.take(received, unit['window_at'], axis=0).reshape(-1, model_width)  10 us
    eq x8, other arithmetic, outgoing(): slots == unit['window_at'][entry]  5.17 us
  transfers between devices with their start and end apart: 6, of which 1 were waited for; matrix products, arithmetic and copies ran while one was open for 6% of the time, Pallas kernels for 0%

profile of v4, /device:TPU:15, one launch (start us, length us, event | category | flops | bytes accessed | tf_op | source)
XLA Modules:
  0.0 242.2 jit_solution(14708044992878195190)
XLA Ops:
  0.0 0.8 reshape_squeeze.9
  0.9 0.7 collective-permute-start.3
  1.7 1.1 dynamic-slice_bitcast_fusion
  2.8 0.5 collective-permute-start
  3.9 0.7 fusion.137
  4.6 0.7 fusion.135
  5.3 0.7 fusion.103
  6.0 0.7 fusion.102
  6.8 0.6 fusion.104
  7.5 0.6 fusion.105
  8.2 0.7 fusion.99
  9.0 0.7 fusion.98
  9.7 0.6 fusion.100
  10.4 0.6 fusion.101
  11.1 0.7 broadcast_select_fusion.12
  11.8 1.1 bitcast_select_fusion.8
  14.7 1.1 convolution_convert_fusion.7.refs_3_
  15.8 1.0 convolution_convert_fusion.6.refs_3_
  16.8 1.6 broadcast_select_fusion
  18.5 21.6 %shard_map.64 = (bf16[4,256,512]{2,1,0:T(8,128)(2,1)S(1)}, bf16[4,256,1536]{2,1,0:T(8,128)(2,1)}) custom-call(bf16[256,512]{1,0:T(8,128)(2,1)S(1)} %get-tuple-element.95.refs_0_.refs_1_, bf16[256,512]{1,0:T(8,128)(2,1)S(1)} %get-tuple-element.95.refs_0_.refs_1_, bf16[256,512]{1,0:T(8,128)(2,1)S(1)} %get-tuple-element.94.refs_2_.refs_4_, ...), custom_call_target="tpu_custom_call" | custom-call | flops 1610612736 | bytes 1048577 | tf_op jit(solution)/shard_map/pallas_call | solution.py:268
  40.1 2.4 %slice_bitcast_fusion = (bf16[256,1536]{1,0:T(8,128)(2,1)S(1)}, bf16[256,1536]{1,0:T(8,128)(2,1)S(1)}, bf16[256,1536]{1,0:T(8,128)(2,1)S(1)}, bf16[256,1536]{1,0:T(8,128)(2,1)S(1)}) fusion(bf16[4,256,1536]{2,1,0:T(8,128)(2,1)} %get-tuple-element.26), kind=kLoop, calls=%fused_computation.67 | loop fusion | bytes 6291456 | tf_op jit(solution)/shard_map/unstack | solution.py:405
  42.6 0.9 slice.267
  43.4 0.7 slice.257.refs_0_
  44.2 0.9 slice.258
  45.0 0.7 slice.250.refs_0_
  45.8 0.9 slice.251
  46.6 0.7 slice.244.refs_0_
  47.3 0.9 slice.245
  48.2 2.5 %gather_fusion = bf16[2,128,512]{2,1,0:T(8,128)(2,1)} fusion(bf16[8,128,512]{2,1,0:T(8,128)(2,1)} %bitcast.329, s32[1024]{0:T(1024)S(1)} %pad_clamp_fusion.3), kind=kCustom, calls=%fused_computation.clone | custom fusion | bytes 524296 | tf_op jit(solution)/shard_map/jit(_take)/gather | solution.py:317
  50.7 1.1 broadcast_select_fusion.7
  51.8 0.4 convolution_convert_fusion.3
  53.1 40.6 %shard_map.65 = (f32[256,512]{1,0:T(8,128)S(1)}, f32[512,512]{1,0:T(8,128)S(1)}, f32[512,512]{1,0:T(8,128)S(1)}, bf16[4,256,512]{2,1,0:T(8,128)(2,1)S(1)}, bf16[...) custom-call(bf16[256,512]{1,0:T(8,128)(2,1)S(1)} %copy-done.12, bf16[512,512]{1,0:T(8,128)(2,1)S(1)} %get-tuple-element.91.refs_1_, ...), custom_call_target="tpu_custom_call" | custom-call | flops 5368709120 | bytes 3145729 | tf_op jit(solution)/shard_map/pallas_call | solution.py:268
  93.8 1.5 fusion.32
  95.3 2.5 %gather_fusion.1 = bf16[2,128,512]{2,1,0:T(8,128)(2,1)} fusion(bf16[8,128,512]{2,1,0:T(8,128)(2,1)} %bitcast.330, s32[1024]{0:T(1024)S(1)} %pad_clamp_fusion.2), kind=kCustom, calls=%fused_computation.1.clone | custom fusion | bytes 524296 | tf_op jit(solution)/shard_map/jit(_take)/gather | solution.py:317
  97.8 1.1 broadcast_select_fusion.6
  100.1 1.2 fusion.7.refs_4_
  101.4 29.9 %shard_map.66 = (f32[256,512]{1,0:T(8,128)S(1)}, f32[512,512]{1,0:T(8,128)S(1)}, f32[512,512]{1,0:T(8,128)S(1)}, bf16[4,256,512]{2,1,0:T(8,128)(2,1)S(1)}) custom-call(bf16[256,512]{1,0:T(8,128)(2,1)S(1)} %copy-done.11, bf16[512,512]{1,0:T(8,128)(2,1)S(1)} %get-tuple-element.87.refs_1_, bf16[512,512]{1,0:T(8,128)(2,1)S(1)} %get-tuple-element.86.refs_2_, ...), custom_call_target="tpu_custom_call" | custom-call | flops 5368709120 | bytes 4194305 | tf_op jit(solution)/shard_map/pallas_call | solution.py:268
  131.5 0.8 copy-done.2
  132.4 1.3 fusion.30
  133.7 0.7 convert.32
  134.5 2.5 %gather_fusion.2 = bf16[2,128,512]{2,1,0:T(8,128)(2,1)} fusion(bf16[8,128,512]{2,1,0:T(8,128)(2,1)} %bitcast.351, s32[1024]{0:T(1024)S(1)} %pad_clamp_fusion.1), kind=kCustom, calls=%fused_computation.2.clone | custom fusion | bytes 524296 | tf_op jit(solution)/shard_map/jit(_take)/gather | solution.py:317
  137.0 1.2 broadcast_select_fusion.5
  138.9 0.7 fusion.124
  140.1 1.2 fusion.47
  141.9 1.2 fusion.5.refs_4_
  143.5 29.7 %shard_map.67 = (f32[256,512]{1,0:T(8,128)S(1)}, f32[512,512]{1,0:T(8,128)S(1)}, f32[512,512]{1,0:T(8,128)S(1)}, bf16[4,256,512]{2,1,0:T(8,128)(2,1)S(1)}) custom-call(bf16[256,512]{1,0:T(8,128)(2,1)S(1)} %copy-done.10, bf16[512,512]{1,0:T(8,128)(2,1)S(1)} %get-tuple-element.89.refs_1_, bf16[512,512]{1,0:T(8,128)(2,1)S(1)} %get-tuple-element.88.refs_2_, ...), custom_call_target="tpu_custom_call" | custom-call | flops 5368709120 | bytes 4194305 | tf_op jit(solution)/shard_map/pallas_call | solution.py:268
  173.4 1.5 fusion.26
  174.9 2.5 %gather_fusion.3 = bf16[2,128,512]{2,1,0:T(8,128)(2,1)} fusion(bf16[8,128,512]{2,1,0:T(8,128)(2,1)} %bitcast.350, s32[1024]{0:T(1024)S(1)} %pad_clamp_fusion), kind=kCustom, calls=%fused_computation.3.clone | custom fusion | bytes 524296 | tf_op jit(solution)/shard_map/jit(_take)/gather | solution.py:317
  177.4 1.2 broadcast_select_fusion.4
  179.3 0.4 copy-done.25
  179.9 0.7 fusion.123
  181.1 1.2 fusion.60
  182.9 1.2 fusion.3.refs_4_
  184.5 26.7 %shard_map.68 = (f32[256,512]{1,0:T(8,128)S(1)}, f32[512,512]{1,0:T(8,128)S(1)}, f32[512,512]{1,0:T(8,128)S(1)}, bf16[4,256,512]{2,1,0:T(8,128)(2,1)S(1)}) custom-call(bf16[256,512]{1,0:T(8,128)(2,1)S(1)} %slice.266.refs_0_, bf16[512,512]{1,0:T(8,128)(2,1)S(1)} %get-tuple-element.85.refs_1_, bf16[512,512]{1,0:T(8,128)(2,1)S(1)} %get-tuple-element.84.refs_2_, ...), custom_call_target="tpu_custom_call" | custom-call | flops 5368709120 | bytes 4194305 | tf_op jit(solution)/shard_map/pallas_call | solution.py:268
  211.4 0.5 fusion.24
  211.9 0.9 copy-done.7
  213.6 0.5 fusion.1.refs_0_
  214.1 19.3 %shard_map.69 = bf16[4,256,512]{2,1,0:T(8,128)(2,1)S(1)} custom-call(bf16[4,256,512]{2,1,0:T(8,128)(2,1)S(1)} %fusion.1.refs_0_), custom_call_target="tpu_custom_call" | custom-call | bytes 4194305 | tf_op jit(solution)/shard_map/pallas_call | solution.py:268
  233.6 0.6 fusion.8
  234.8 0.8 fusion.122
  235.7 0.7 select_bitcast_fusion.5
  236.6 2.9 %collective-permute-start.5 = (bf16[2,256,512]{2,1,0:T(8,128)(2,1)S(1)}, bf16[2,256,512]{2,1,0:T(8,128)(2,1)S(1)}, u32[]{:S(2)}, u32[]{:S(2)}) collective-permute-start(bf16[2,256,512]{2,1,0:T(8,128)(2,1)S(1)} %pad_maximum_fusion.6), channel_id=1, source_target_pairs={{0,64},{64,0},{1,65},{65,1},{2,66},{66,2},{3,67},{67,3},{4,68},{68... | collective-permute-start | bytes 1572872 | tf_op jit(solution)/shard_map/ppermute | solution.py:290
  239.4 1.5 collective-permute-done.5
  241.1 1.0 copy.15
  (192 shorter events, 11.9 us)
Async XLA Ops:
  0.9 3.0 %collective-permute-start.3 = (s32[2,2]{1,0:T(2,128)S(1)}, s32[2,2]{1,0:T(2,128)S(1)}, u32[]{:S(2)}, u32[]{:S(2)}) collective-permute-start(s32[2,2]{1,0:T(2,128)S(1)} %bitcast.354), channel_id=1, source_target_pairs={{0,64},{64,0},{1,65},{65,1},{2,66},{66,2},{3,67},{67,3},{4,68},{68... | collective-permute-start | bytes 56 | tf_op jit(solution)/shard_map/ppermute | solution.py:290
  1.6 9.5 %collective-permute-start.1 = (f32[512]{0:T(512)}, f32[512]{0:T(512)S(1)}, u32[]{:S(2)}, u32[]{:S(2)}) collective-permute-start(f32[512]{0:T(512)} %bitcast.352), channel_id=1, source_target_pairs={{0,64},{64,0},{1,65},{65,1},{2,66},{66,2},{3,67},{67,3},{4,68},{68... | collective-permute-start | bytes 6152 | tf_op jit(solution)/shard_map/ppermute | solution.py:290
  2.8 9.1 %collective-permute-start = (bf16[2,256,512]{2,1,0:T(8,128)(2,1)S(1)}, bf16[2,256,512]{2,1,0:T(8,128)(2,1)S(1)}, u32[]{:S(2)}, u32[]{:S(2)}) collective-permute-start(bf16[2,256,512]{2,1,0:T(8,128)(2,1)S(1)} %dynamic-slice_bitcast_fusion), channel_id=1, source_target_pairs={{0,64},{64,0},{1,65},{65,1},{2,66},{66,2},{3,67},{67,3},{4,68},{68... | collective-permute-start | bytes 1572872 | tf_op jit(solution)/shard_map/ppermute | solution.py:290
  3.3 11.2 %collective-permute-start.4 = (bf16[512,512]{1,0:T(8,128)(2,1)}, bf16[512,512]{1,0:T(8,128)(2,1)S(1)}, u32[]{:S(2)}, u32[]{:S(2)}) collective-permute-start(bf16[512,512]{1,0:T(8,128)(2,1)} %bitcast.355), channel_id=1, source_target_pairs={{0,64},{64,0},{1,65},{65,1},{2,66},{66,2},{3,67},{67,3},{4,68},{68... | collective-permute-start | bytes 1572872 | tf_op jit(solution)/shard_map/ppermute | solution.py:290
  3.4 13.4 %collective-permute-start.2 = (bf16[512,1536]{1,0:T(8,128)(2,1)}, bf16[512,1536]{1,0:T(8,128)(2,1)}, u32[]{:S(2)}, u32[]{:S(2)}) collective-permute-start(bf16[512,1536]{1,0:T(8,128)(2,1)} %bitcast.339), channel_id=1, source_target_pairs={{0,64},{64,0},{1,65},{65,1},{2,66},{66,2},{3,67},{67,3},{4,68},{68... | collective-permute-start | bytes 4718600 | tf_op jit(solution)/shard_map/ppermute | solution.py:290
  13.0 1.2 copy-start.26
  13.0 1.5 copy-start.23
  13.0 1.6 copy-start.43
  13.0 1.7 copy-start.44
  14.2 4.2 %copy-start.13 = (bf16[256,512]{1,0:T(8,128)(2,1)}, bf16[256,512]{1,0:T(8,128)(2,1)S(1)}, u32[]{:S(2)}) copy-start(bf16[256,512]{1,0:T(8,128)(2,1)S(1)} %get-tuple-element.92.refs_4_.refs_6_) | copy-start | bytes 786436
  14.2 4.2 %copy-start.15 = (bf16[256,512]{1,0:T(8,128)(2,1)}, bf16[256,512]{1,0:T(8,128)(2,1)S(1)}, u32[]{:S(2)}) copy-start(bf16[256,512]{1,0:T(8,128)(2,1)S(1)} %get-tuple-element.93.refs_3_.refs_5_) | copy-start | bytes 786436
  14.2 2.6 %copy-start.38 = (bf16[1,512,1536]{2,1,0:T(8,128)(2,1)S(1)}, bf16[1,512,1536]{2,1,0:T(8,128)(2,1)}, u32[]{:S(2)}) copy-start(bf16[1,512,1536]{2,1,0:T(8,128)(2,1)} %param.9) | copy-start | bytes 4718596
  14.5 4.0 %copy-start.17 = (bf16[256,512]{1,0:T(8,128)(2,1)}, bf16[256,512]{1,0:T(8,128)(2,1)S(1)}, u32[]{:S(2)}) copy-start(bf16[256,512]{1,0:T(8,128)(2,1)S(1)} %get-tuple-element.94.refs_2_.refs_4_) | copy-start | bytes 786436
  14.5 2.3 copy-start.47
  40.1 2.4 %copy-start.19 = (bf16[4,256,512]{2,1,0:T(8,128)(2,1)}, bf16[4,256,512]{2,1,0:T(8,128)(2,1)S(1)}, u32[]{:S(2)}) copy-start(bf16[4,256,512]{2,1,0:T(8,128)(2,1)S(1)} %get-tuple-element.27) | copy-start | bytes 3145732
  50.7 1.6 copy-start.37
  51.8 1.0 copy-start.12
  51.8 1.0 copy-start.14
  51.8 1.1 copy-start.16
  51.8 1.2 copy-start.18
  51.8 1.2 copy-start.22
  93.7 1.7 copy-start.8
  93.7 1.7 copy-start.20
  93.8 1.5 copy-start.28
  97.8 1.6 copy-start.41
  97.8 1.6 copy-start.36
  100.1 1.3 copy-start.11
  100.1 1.3 copy-start.21
  131.3 1.0 copy-start.2
  131.3 1.1 copy-start.4
  131.5 3.0 %copy-start.29 = (bf16[512,1024]{1,0:T(8,128)(2,1)}, bf16[512,1024]{1,0:T(8,128)(2,1)S(1)}, u32[]{:S(2)}) copy-start(bf16[512,1024]{1,0:T(8,128)(2,1)S(1)} %maximum_convert_fusion.1) | copy-start | bytes 3145732
  131.5 2.3 copy-start.9
  137.0 1.7 copy-start.3
  137.0 1.8 copy-start.24
  137.0 1.8 slice-start
  137.0 1.8 copy-start.42
  138.8 1.0 copy-start.40
  138.9 1.2 copy-start.35
  141.3 1.8 copy-start.32
  141.9 1.3 copy-start.45
  141.9 1.3 copy-start.48
  141.9 1.6 copy-start.10
  173.3 1.6 copy-start
  173.3 1.6 copy-start.6
  173.4 1.5 copy-start.30
  177.4 1.6 copy-start.5
  177.4 1.7 copy-start.1
  178.6 1.1 copy-start.25
  178.6 1.3 slice-start.1
  179.9 1.0 copy-start.39
  179.9 1.2 copy-start.34
  182.9 1.3 copy-start.46
  182.9 1.3 copy-start.49
  211.4 1.5 copy-start.31
  211.4 1.4 copy-start.7
  214.1 19.5 %slice-start.3 = ((bf16[512,1024]{1,0:T(8,128)(2,1)}), bf16[256,1024]{1,0:T(8,128)(2,1)S(1)}, s32[]{:S(2)}) async-start(bf16[512,1024]{1,0:T(8,128)(2,1)} %copy-done.31), calls=%async_computation.3 | async-start | bytes 1048576 | tf_op jit(solution)/shard_map/slice | solution.py:338
  233.6 1.0 copy-start.27
  233.6 1.2 slice-start.2
  234.8 0.9 copy-start.33
  236.6 4.4 %collective-permute-start.5 = (bf16[2,256,512]{2,1,0:T(8,128)(2,1)S(1)}, bf16[2,256,512]{2,1,0:T(8,128)(2,1)S(1)}, u32[]{:S(2)}, u32[]{:S(2)}) collective-permute-start(bf16[2,256,512]{2,1,0:T(8,128)(2,1)S(1)} %pad_maximum_fusion.6), channel_id=1, source_target_pairs={{0,64},{64,0},{1,65},{65,1},{2,66},{66,2},{3,67},{67,3},{4,68},{68... | collective-permute-start | bytes 1572872 | tf_op jit(solution)/shard_map/ppermute | solution.py:290

commit v5 on v3

--- a/solution.py
+++ b/solution.py
@@ -85,10 +85,10 @@
     else:
         begin = 0
         for edge in sorted(hooks):
-            lax.fori_loop(begin, edge, head, 0, unroll=2)
+            lax.fori_loop(begin, edge, head, 0, unroll=4)
             hooks[edge]()
             begin = edge
-        lax.fori_loop(begin, heads, head, 0, unroll=2)
+        lax.fori_loop(begin, heads, head, 0, unroll=4)
 
 
 def exchange_start(spreads, payload_refs, out_refs, send_sems, recv_sems):
@@ -208,9 +208,7 @@
         hooks = {}
         if not any(spreads):
             heads = attention_in[0].shape[1] // HD
-            for which in range(count):
-                edge = (which + 1) * heads // (count + 1)
-                hooks[edge] = functools.partial(relay, [which])
+            hooks[heads // 2] = functools.partial(relay, list(range(count)))
         attention_body(*attention_in, *attention_out, hooks)
     else:
         relay(list(range(count)))

time: 236 us -> 237 us (level)
  no operation moved by 1% of the time
where the time goes in v5:
time: 237 us; the launch traced here: 233 us
  Pallas kernels  164 us (69%)
  local copies, waits for them, and re-layouts  24.5 us (10%)
  other arithmetic  18.4 us (8%)
  matrix products  17.7 us (7%)
  starting transfers between devices  5.41 us (2%)
    pallas_call x6, Pallas kernels, fused_step(): pl.pallas_call(functools.partial(fused_kernel, tuple(spreads), bool(atten...  164 us
    unnamed x54, local copies, waits for them, and re-layouts  10.8 us
    dot_general x4, matrix products, attach(): jnp.dot(fetched, weight_in[:, model_width:], preferred_element_type=jnp.f...  5.69 us
    ppermute x6, starting transfers between devices, swap_cores(): return lax.ppermute(value, 'pipe', [(0, 1), (1, 0)])  5.41 us
    eq x8, other arithmetic, outgoing(): slots == unit['window_at'][entry]  5.06 us
  transfers between devices with their start and end apart: 6, of which 1 were waited for; matrix products, arithmetic and copies ran while one was open for 5% of the time, Pallas kernels for 9%

profile of v5, /device:TPU:15, one launch (start us, length us, event | category | flops | bytes accessed | tf_op | source)
XLA Modules:
  0.0 232.7 jit_solution(7354549323441947147)
XLA Ops:
  0.0 0.8 reshape_squeeze.9
  1.0 0.7 collective-permute-start.3
  1.8 1.1 dynamic-slice_bitcast_fusion
  2.9 0.5 collective-permute-start
  4.0 0.7 fusion.137
  4.7 0.7 fusion.135
  5.4 0.7 fusion.103
  6.1 0.6 fusion.102
  6.8 0.6 fusion.104
  7.6 0.6 fusion.105
  8.3 0.6 fusion.99
  9.0 0.6 fusion.98
  9.7 0.7 fusion.100
  10.4 0.6 fusion.101
  11.1 0.7 broadcast_select_fusion.13
  13.1 20.0 %shard_map.64 = bf16[4,256,512]{2,1,0:T(8,128)(2,1)S(1)} custom-call(bf16[256,512]{1,0:T(8,128)(2,1)S(1)} %get-tuple-element.87.refs_0_), custom_call_target="tpu_custom_call" | custom-call | bytes 1048577 | tf_op jit(solution)/shard_map/pallas_call | solution.py:236
  33.1 0.6 gather_fusion
  34.1 0.7 copy-done.24
  35.5 0.7 copy-done.20
  36.2 1.6 broadcast_select_fusion.1
  37.8 0.6 convolution_convert_fusion.3
  38.4 0.6 convolution_convert_fusion.2
  39.0 0.7 copy-done.12
  39.7 0.6 convolution_convert_fusion
  40.6 0.6 convolution_convert_fusion.1
  41.5 0.9 copy-done.15
  43.0 39.8 %shard_map.65 = (f32[256,512]{1,0:T(8,128)S(1)}, f32[512,512]{1,0:T(8,128)S(1)}, f32[512,512]{1,0:T(8,128)S(1)}, bf16[4,256,512]{2,1,0:T(8,128)(2,1)S(1)}, bf16[...) custom-call(bf16[256,512]{1,0:T(8,128)(2,1)S(1)} %slice.241.refs_0_, ...), custom_call_target="tpu_custom_call" | custom-call | flops 5368709120 | bytes 3145729 | tf_op jit(solution)/shard_map/pallas_call | solution.py:236
  83.0 1.3 fusion.32
  84.2 0.6 gather_fusion.1
  84.9 1.7 convolution_convert_fusion.6
  86.6 1.1 fusion.134
  88.3 1.2 fusion.7.refs_4_
  89.6 29.9 %shard_map.66 = (f32[256,512]{1,0:T(8,128)S(1)}, f32[512,512]{1,0:T(8,128)S(1)}, f32[512,512]{1,0:T(8,128)S(1)}, bf16[4,256,512]{2,1,0:T(8,128)(2,1)S(1)}) custom-call(bf16[256,512]{1,0:T(8,128)(2,1)S(1)} %slice.250.refs_0_, bf16[512,512]{1,0:T(8,128)(2,1)S(1)} %get-tuple-element.79.refs_1_, bf16[512,512]{1,0:T(8,128)(2,1)S(1)} %get-tuple-element.78.refs_2_, ...), custom_call_target="tpu_custom_call" | custom-call | flops 5368709120 | bytes 4194305 | tf_op jit(solution)/shard_map/pallas_call | solution.py:236
  119.7 1.6 copy-done.4
  121.3 1.3 fusion.30
  122.6 1.8 gather_fusion.2
  124.5 1.8 convolution_convert_fusion.5
  126.6 0.7 fusion.124
  127.8 1.2 fusion.47
  129.6 1.2 fusion.5.refs_4_
  130.8 1.4 convolution_convert_fusion.9.refs_3_
  132.2 28.9 %shard_map.67 = (f32[256,512]{1,0:T(8,128)S(1)}, f32[512,512]{1,0:T(8,128)S(1)}, f32[512,512]{1,0:T(8,128)S(1)}, bf16[4,256,512]{2,1,0:T(8,128)(2,1)S(1)}) custom-call(bf16[256,512]{1,0:T(8,128)(2,1)S(1)} %slice.257.refs_0_, bf16[512,512]{1,0:T(8,128)(2,1)S(1)} %get-tuple-element.81.refs_1_, bf16[512,512]{1,0:T(8,128)(2,1)S(1)} %get-tuple-element.80.refs_2_, ...), custom_call_target="tpu_custom_call" | custom-call | flops 5368709120 | bytes 4194305 | tf_op jit(solution)/shard_map/pallas_call | solution.py:236
  161.2 1.3 copy-done.1
  162.5 0.5 fusion.26
  163.0 0.5 copy-done.18
  163.5 1.8 gather_fusion.3
  165.4 1.7 convolution_convert_fusion.4
  167.3 1.2 copy-done.6
  168.6 0.7 fusion.123
  169.7 1.2 fusion.60
  171.5 1.2 fusion.3.refs_4_
  172.7 1.4 convolution_convert_fusion.8.refs_3_
  174.1 27.6 %shard_map.68 = (f32[256,512]{1,0:T(8,128)S(1)}, f32[512,512]{1,0:T(8,128)S(1)}, f32[512,512]{1,0:T(8,128)S(1)}, bf16[4,256,512]{2,1,0:T(8,128)(2,1)S(1)}) custom-call(bf16[256,512]{1,0:T(8,128)(2,1)S(1)} %slice.266.refs_0_, bf16[512,512]{1,0:T(8,128)(2,1)S(1)} %get-tuple-element.77.refs_1_, bf16[512,512]{1,0:T(8,128)(2,1)S(1)} %get-tuple-element.76.refs_2_, ...), custom_call_target="tpu_custom_call" | custom-call | flops 5368709120 | bytes 4194305 | tf_op jit(solution)/shard_map/pallas_call | solution.py:236
  201.8 1.3 copy-done.2
  203.1 0.5 fusion.24
  203.5 0.5 copy-done.19
  204.8 0.5 fusion.1.refs_0_
  205.3 18.0 %shard_map.69 = bf16[4,256,512]{2,1,0:T(8,128)(2,1)S(1)} custom-call(bf16[4,256,512]{2,1,0:T(8,128)(2,1)S(1)} %fusion.1.refs_0_), custom_call_target="tpu_custom_call" | custom-call | bytes 4194305 | tf_op jit(solution)/shard_map/pallas_call | solution.py:236
  223.5 0.6 fusion.8
  224.7 0.8 fusion.122
  225.5 0.7 select_bitcast_fusion.5
  226.3 3.6 %collective-permute-start.5 = (bf16[2,256,512]{2,1,0:T(8,128)(2,1)S(1)}, bf16[2,256,512]{2,1,0:T(8,128)(2,1)S(1)}, u32[]{:S(2)}, u32[]{:S(2)}) collective-permute-start(bf16[2,256,512]{2,1,0:T(8,128)(2,1)S(1)} %pad_maximum_fusion.6), channel_id=1, source_target_pairs={{0,64},{64,0},{1,65},{65,1},{2,66},{66,2},{3,67},{67,3},{4,68},{68... | collective-permute-start | bytes 1572872 | tf_op jit(solution)/shard_map/ppermute | solution.py:258
  230.0 1.5 collective-permute-done.5
  231.7 1.0 copy.15
  (153 shorter events, 10.6 us)
Async XLA Ops:
  0.0 11.8 %copy-start.21 = (bf16[1,4,256,512]{3,2,1,0:T(8,128)(2,1)S(1)}, bf16[1,4,256,512]{3,2,1,0:T(8,128)(2,1)}, u32[]{:S(2)}) copy-start(bf16[1,4,256,512]{3,2,1,0:T(8,128)(2,1)} %param.8) | copy-start | bytes 3145732
  1.0 3.0 %collective-permute-start.3 = (s32[2,2]{1,0:T(2,128)S(1)}, s32[2,2]{1,0:T(2,128)S(1)}, u32[]{:S(2)}, u32[]{:S(2)}) collective-permute-start(s32[2,2]{1,0:T(2,128)S(1)} %bitcast.354), channel_id=1, source_target_pairs={{0,64},{64,0},{1,65},{65,1},{2,66},{66,2},{3,67},{67,3},{4,68},{68... | collective-permute-start | bytes 56 | tf_op jit(solution)/shard_map/ppermute | solution.py:258
  1.7 9.4 %collective-permute-start.1 = (f32[512]{0:T(512)}, f32[512]{0:T(512)S(1)}, u32[]{:S(2)}, u32[]{:S(2)}) collective-permute-start(f32[512]{0:T(512)} %bitcast.352), channel_id=1, source_target_pairs={{0,64},{64,0},{1,65},{65,1},{2,66},{66,2},{3,67},{67,3},{4,68},{68... | collective-permute-start | bytes 6152 | tf_op jit(solution)/shard_map/ppermute | solution.py:258
  2.9 9.0 %collective-permute-start = (bf16[2,256,512]{2,1,0:T(8,128)(2,1)S(1)}, bf16[2,256,512]{2,1,0:T(8,128)(2,1)S(1)}, u32[]{:S(2)}, u32[]{:S(2)}) collective-permute-start(bf16[2,256,512]{2,1,0:T(8,128)(2,1)S(1)} %dynamic-slice_bitcast_fusion), channel_id=1, source_target_pairs={{0,64},{64,0},{1,65},{65,1},{2,66},{66,2},{3,67},{67,3},{4,68},{68... | collective-permute-start | bytes 1572872 | tf_op jit(solution)/shard_map/ppermute | solution.py:258
  3.4 30.7 %collective-permute-start.4 = (bf16[512,512]{1,0:T(8,128)(2,1)}, bf16[512,512]{1,0:T(8,128)(2,1)}, u32[]{:S(2)}, u32[]{:S(2)}) collective-permute-start(bf16[512,512]{1,0:T(8,128)(2,1)} %bitcast.355), channel_id=1, source_target_pairs={{0,64},{64,0},{1,65},{65,1},{2,66},{66,2},{3,67},{67,3},{4,68},{68... | collective-permute-start | bytes 1572872 | tf_op jit(solution)/shard_map/ppermute | solution.py:258
  3.5 32.0 %collective-permute-start.2 = (bf16[512,1536]{1,0:T(8,128)(2,1)}, bf16[512,1536]{1,0:T(8,128)(2,1)}, u32[]{:S(2)}, u32[]{:S(2)}) collective-permute-start(bf16[512,1536]{1,0:T(8,128)(2,1)} %bitcast.339), channel_id=1, source_target_pairs={{0,64},{64,0},{1,65},{65,1},{2,66},{66,2},{3,67},{67,3},{4,68},{68... | collective-permute-start | bytes 4718600 | tf_op jit(solution)/shard_map/ppermute | solution.py:258
  11.9 1.2 copy-start.7
  11.9 21.9 %copy-start.10 = (bf16[2,256,512]{2,1,0:T(8,128)(2,1)}, bf16[2,256,512]{2,1,0:T(8,128)(2,1)S(1)}, u32[]{:S(2)}) copy-start(bf16[2,256,512]{2,1,0:T(8,128)(2,1)S(1)} %get-tuple-element.73) | copy-start | bytes 1572868
  13.1 21.0 %copy-start.23 = (bf16[4,256,512]{2,1,0:T(8,128)(2,1)S(1)}, bf16[4,256,512]{2,1,0:T(8,128)(2,1)}, u32[]{:S(2)}) copy-start(bf16[4,256,512]{2,1,0:T(8,128)(2,1)} %param.13) | copy-start | bytes 3145732
  33.7 1.0 copy-start.24
  34.7 1.4 copy-start.20
  37.8 2.8 %copy-start = (bf16[512,1536]{1,0:T(8,128)(2,1)}, bf16[512,1536]{1,0:T(8,128)(2,1)S(1)}, u32[]{:S(2)}) copy-start(bf16[512,1536]{1,0:T(8,128)(2,1)S(1)} %get-tuple-element.71) | copy-start | bytes 4718596
  37.8 45.2 %copy-start.3 = (bf16[512,1536]{1,0:T(8,128)(2,1)}, bf16[512,1536]{1,0:T(8,128)(2,1)S(1)}, u32[]{:S(2)}) copy-start(bf16[512,1536]{1,0:T(8,128)(2,1)S(1)} %get-tuple-element.70) | copy-start | bytes 4718596
  38.4 1.3 copy-start.12
  39.7 0.9 copy-start.13
  40.6 0.9 copy-start.14
  41.5 0.9 copy-start.15
  41.5 1.4 slice-start
  82.9 1.3 copy-start.16
  84.9 2.8 %slice-start.1 = ((bf16[256,1536]{1,0:T(8,128)(2,1)}), bf16[256,1024]{1,0:T(8,128)(2,1)S(1)}, s32[]{:S(2)}) async-start(bf16[256,1536]{1,0:T(8,128)(2,1)} %copy-done.13), calls=%async_computation.1 | async-start | bytes 1048576 | tf_op jit(solution)/shard_map/slice | solution.py:280
  119.5 1.8 copy-start.4
  119.7 2.9 %copy-start.17 = (bf16[512,1024]{1,0:T(8,128)(2,1)}, bf16[512,1024]{1,0:T(8,128)(2,1)S(1)}, u32[]{:S(2)}) copy-start(bf16[512,1024]{1,0:T(8,128)(2,1)S(1)} %maximum_convert_fusion.1) | copy-start | bytes 3145732
  124.5 2.0 copy-start.5
  124.5 2.0 copy-start.8
  124.5 2.0 slice-start.4
  126.5 1.0 copy-start.22
  126.5 1.2 slice-start.3
  129.5 1.3 copy-start.25
  161.1 1.4 copy-start.1
  162.5 1.0 copy-start.18
  165.3 2.0 slice-start.5
  167.1 1.4 copy-start.6
  167.1 1.5 copy-start.9
  168.6 1.0 slice-start.2
  171.5 1.3 copy-start.26
  201.7 1.4 copy-start.2
  203.1 1.0 copy-start.19
  205.3 18.2 %slice-start.7 = ((bf16[512,1024]{1,0:T(8,128)(2,1)}), bf16[256,1024]{1,0:T(8,128)(2,1)S(1)}, s32[]{:S(2)}) async-start(bf16[512,1024]{1,0:T(8,128)(2,1)} %copy-done.19), calls=%async_computation.7 | async-start | bytes 1048576 | tf_op jit(solution)/shard_map/slice | solution.py:309
  223.5 1.0 copy-start.11
  223.5 1.2 slice-start.6
  226.3 5.2 %collective-permute-start.5 = (bf16[2,256,512]{2,1,0:T(8,128)(2,1)S(1)}, bf16[2,256,512]{2,1,0:T(8,128)(2,1)S(1)}, u32[]{:S(2)}, u32[]{:S(2)}) collective-permute-start(bf16[2,256,512]{2,1,0:T(8,128)(2,1)S(1)} %pad_maximum_fusion.6), channel_id=1, source_target_pairs={{0,64},{64,0},{1,65},{65,1},{2,66},{66,2},{3,67},{67,3},{4,68},{68... | collective-permute-start | bytes 1572872 | tf_op jit(solution)/shard_map/ppermute | solution.py:258

commit v6 on v5

--- a/solution.py
+++ b/solution.py
@@ -211,7 +211,8 @@
             hooks[heads // 2] = functools.partial(relay, list(range(count)))
         attention_body(*attention_in, *attention_out, hooks)
     else:
-        relay(list(range(count)))
+        for which in range(count):
+            relay([which])
     finish()
 
 
@@ -362,7 +363,14 @@
     ]
     results = {}
     ids = iter(range(len(order) + 2))
-    (first_received,) = fused_step((), [units[0]["normed"]], [False], next(ids))
+    first_rows = units[0]["normed"].shape[0] // 2
+    first_parts = fused_step(
+        (),
+        [units[0]["normed"][:first_rows], units[0]["normed"][first_rows:]],
+        [False, False],
+        next(ids),
+    )
+    first_received = jnp.concatenate(first_parts, axis=1)
     attach(units[0], first_received, params[order[0][0]][2])
     pending = None
     for step, (section, j) in enumerate(order):

time: 237 us -> 238 us (level)
    unnamed x54 -> x52, local copies, waits for them, and re-layouts: 10.8 us -> 9.5 us
  transfers between devices with their start and end apart: 6 -> 6, of which waited for: 1 -> 1; matrix products, arithmetic and copies ran while one was open for 5% -> 6% of each run, Pallas kernels for 9% -> 8%
where the time goes in v6:
time: 238 us; the launch traced here: 234 us
  Pallas kernels  166 us (70%)
  local copies, waits for them, and re-layouts  23.2 us (10%)
  matrix products  19.7 us (8%)
  other arithmetic  18.5 us (8%)
  starting transfers between devices  4.2 us (2%)
    pallas_call x6, Pallas kernels, fused_step(): pl.pallas_call(functools.partial(fused_kernel, tuple(spreads), bool(atten...  166 us
    unnamed x52, local copies, waits for them, and re-layouts  9.5 us
    dot_general x4, matrix products, attach(): jnp.dot(fetched, weight_in[:, model_width:], preferred_element_type=jnp.f...  5.69 us
    dot_general x4, matrix products, shards(): jnp.dot(grad_out, weight_out.T, preferred_element_type=jnp.float32)  5.46 us
    eq x8, other arithmetic, outgoing(): slots == unit['window_at'][entry]  5.11 us
  transfers between devices with their start and end apart: 6, of which 1 were waited for; matrix products, arithmetic and copies ran while one was open for 6% of the time, Pallas kernels for 8%

profile of v6, /device:TPU:15, one launch (start us, length us, event | category | flops | bytes accessed | tf_op | source)
XLA Modules:
  0.0 233.8 jit_solution(2705305933074959356)
XLA Ops:
  0.0 0.8 reshape_squeeze.9
  1.0 0.7 collective-permute-start.3
  1.8 1.1 dynamic-slice_bitcast_fusion
  2.9 0.5 collective-permute-start
  4.0 0.7 fusion.138
  4.7 0.6 fusion.136
  5.4 0.7 fusion.103
  6.1 0.6 fusion.102
  6.8 0.6 fusion.104
  7.5 0.6 fusion.105
  8.2 0.6 fusion.99
  9.0 0.7 fusion.98
  9.7 0.6 fusion.100
  10.3 0.7 fusion.101
  11.2 0.7 broadcast_select_fusion.13
  13.2 19.1 %shard_map.64 = (bf16[4,128,512]{2,1,0:T(8,128)(2,1)S(1)}, bf16[4,128,512]{2,1,0:T(8,128)(2,1)S(1)}) custom-call(bf16[128,512]{1,0:T(8,128)(2,1)S(1)} %get-tuple-element.103.refs_0_, bf16[128,512]{1,0:T(8,128)(2,1)S(1)} %get-tuple-element.102.refs_1_), custom_call_target="tpu_custom_call" | custom-call | bytes 1048577 | tf_op jit(solution)/shard_map/pallas_call | solution.py:237
  32.4 0.6 gather_fusion
  33.4 1.4 convolution_convert_fusion.11.refs_3_
  34.8 1.3 convolution_convert_fusion.10.refs_3_
  36.2 1.6 broadcast_select_fusion.1
  37.8 0.6 convolution_convert_fusion.3
  38.4 0.6 convolution_convert_fusion.2
  39.0 0.7 copy-done.12
  39.7 0.6 convolution_convert_fusion
  40.6 0.6 convolution_convert_fusion.1
  41.5 0.9 copy-done.15
  43.0 40.0 %shard_map.65 = (f32[256,512]{1,0:T(8,128)S(1)}, f32[512,512]{1,0:T(8,128)S(1)}, f32[512,512]{1,0:T(8,128)S(1)}, bf16[4,256,512]{2,1,0:T(8,128)(2,1)S(1)}, bf16[...) custom-call(bf16[256,512]{1,0:T(8,128)(2,1)S(1)} %slice.249.refs_0_, ...), custom_call_target="tpu_custom_call" | custom-call | flops 5368709120 | bytes 3145729 | tf_op jit(solution)/shard_map/pallas_call | solution.py:237
  83.2 1.3 fusion.32
  84.4 0.6 gather_fusion.1
  85.1 1.7 convolution_convert_fusion.6
  86.8 1.1 fusion.134
  88.5 1.2 fusion.7.refs_4_
  89.8 30.2 %shard_map.66 = (f32[256,512]{1,0:T(8,128)S(1)}, f32[512,512]{1,0:T(8,128)S(1)}, f32[512,512]{1,0:T(8,128)S(1)}, bf16[4,256,512]{2,1,0:T(8,128)(2,1)S(1)}) custom-call(bf16[256,512]{1,0:T(8,128)(2,1)S(1)} %slice.260.refs_0_, bf16[512,512]{1,0:T(8,128)(2,1)S(1)} %get-tuple-element.83.refs_1_, bf16[512,512]{1,0:T(8,128)(2,1)S(1)} %get-tuple-element.82.refs_2_, ...), custom_call_target="tpu_custom_call" | custom-call | flops 5368709120 | bytes 4194305 | tf_op jit(solution)/shard_map/pallas_call | solution.py:237
  120.2 1.6 copy-done.4
  121.8 1.3 fusion.30
  123.1 1.8 gather_fusion.2
  125.0 1.8 convolution_convert_fusion.5
  127.0 0.7 fusion.124
  128.3 1.2 fusion.47
  130.1 1.2 fusion.5.refs_4_
  131.3 1.4 convolution_convert_fusion.9.refs_3_
  132.7 30.0 %shard_map.67 = (f32[256,512]{1,0:T(8,128)S(1)}, f32[512,512]{1,0:T(8,128)S(1)}, f32[512,512]{1,0:T(8,128)S(1)}, bf16[4,256,512]{2,1,0:T(8,128)(2,1)S(1)}) custom-call(bf16[256,512]{1,0:T(8,128)(2,1)S(1)} %slice.267.refs_0_, bf16[512,512]{1,0:T(8,128)(2,1)S(1)} %get-tuple-element.85.refs_1_, bf16[512,512]{1,0:T(8,128)(2,1)S(1)} %get-tuple-element.84.refs_2_, ...), custom_call_target="tpu_custom_call" | custom-call | flops 5368709120 | bytes 4194305 | tf_op jit(solution)/shard_map/pallas_call | solution.py:237
  162.9 1.3 copy-done.1
  164.1 0.5 fusion.26
  164.6 0.5 copy-done.18
  165.1 1.8 gather_fusion.3
  167.0 1.7 convolution_convert_fusion.4
  168.9 1.2 copy-done.6
  170.2 0.7 fusion.123
  171.4 1.2 fusion.60
  173.1 1.2 fusion.3.refs_4_
  174.3 1.4 convolution_convert_fusion.8.refs_3_
  175.7 26.4 %shard_map.68 = (f32[256,512]{1,0:T(8,128)S(1)}, f32[512,512]{1,0:T(8,128)S(1)}, f32[512,512]{1,0:T(8,128)S(1)}, bf16[4,256,512]{2,1,0:T(8,128)(2,1)S(1)}) custom-call(bf16[256,512]{1,0:T(8,128)(2,1)S(1)} %slice.276.refs_0_, bf16[512,512]{1,0:T(8,128)(2,1)S(1)} %get-tuple-element.81.refs_1_, bf16[512,512]{1,0:T(8,128)(2,1)S(1)} %get-tuple-element.80.refs_2_, ...), custom_call_target="tpu_custom_call" | custom-call | flops 5368709120 | bytes 4194305 | tf_op jit(solution)/shard_map/pallas_call | solution.py:237
  202.3 1.3 copy-done.2
  203.6 0.5 fusion.24
  204.0 0.5 copy-done.19
  205.3 0.5 fusion.1.refs_0_
  205.8 19.8 %shard_map.69 = bf16[4,256,512]{2,1,0:T(8,128)(2,1)S(1)} custom-call(bf16[4,256,512]{2,1,0:T(8,128)(2,1)S(1)} %fusion.1.refs_0_), custom_call_target="tpu_custom_call" | custom-call | bytes 4194305 | tf_op jit(solution)/shard_map/pallas_call | solution.py:237
  225.8 0.6 fusion.8
  227.0 0.8 fusion.122
  227.8 0.7 select_bitcast_fusion.5
  228.7 2.4 %collective-permute-start.5 = (bf16[2,256,512]{2,1,0:T(8,128)(2,1)S(1)}, bf16[2,256,512]{2,1,0:T(8,128)(2,1)S(1)}, u32[]{:S(2)}, u32[]{:S(2)}) collective-permute-start(bf16[2,256,512]{2,1,0:T(8,128)(2,1)S(1)} %pad_maximum_fusion.7), channel_id=1, source_target_pairs={{0,64},{64,0},{1,65},{65,1},{2,66},{66,2},{3,67},{67,3},{4,68},{68... | collective-permute-start | bytes 1572872 | tf_op jit(solution)/shard_map/ppermute | solution.py:259
  231.1 1.5 collective-permute-done.5
  232.8 1.0 copy.15
  (153 shorter events, 10.1 us)
Async XLA Ops:
  0.0 11.9 %copy-start.21 = (bf16[1,4,256,512]{3,2,1,0:T(8,128)(2,1)S(1)}, bf16[1,4,256,512]{3,2,1,0:T(8,128)(2,1)}, u32[]{:S(2)}) copy-start(bf16[1,4,256,512]{3,2,1,0:T(8,128)(2,1)} %param.8) | copy-start | bytes 3145732
  1.0 3.0 %collective-permute-start.3 = (s32[2,2]{1,0:T(2,128)S(1)}, s32[2,2]{1,0:T(2,128)S(1)}, u32[]{:S(2)}, u32[]{:S(2)}) collective-permute-start(s32[2,2]{1,0:T(2,128)S(1)} %bitcast.354), channel_id=1, source_target_pairs={{0,64},{64,0},{1,65},{65,1},{2,66},{66,2},{3,67},{67,3},{4,68},{68... | collective-permute-start | bytes 56 | tf_op jit(solution)/shard_map/ppermute | solution.py:259
  1.7 9.5 %collective-permute-start.1 = (f32[512]{0:T(512)}, f32[512]{0:T(512)S(1)}, u32[]{:S(2)}, u32[]{:S(2)}) collective-permute-start(f32[512]{0:T(512)} %bitcast.352), channel_id=1, source_target_pairs={{0,64},{64,0},{1,65},{65,1},{2,66},{66,2},{3,67},{67,3},{4,68},{68... | collective-permute-start | bytes 6152 | tf_op jit(solution)/shard_map/ppermute | solution.py:259
  2.9 9.0 %collective-permute-start = (bf16[2,256,512]{2,1,0:T(8,128)(2,1)S(1)}, bf16[2,256,512]{2,1,0:T(8,128)(2,1)S(1)}, u32[]{:S(2)}, u32[]{:S(2)}) collective-permute-start(bf16[2,256,512]{2,1,0:T(8,128)(2,1)S(1)} %dynamic-slice_bitcast_fusion), channel_id=1, source_target_pairs={{0,64},{64,0},{1,65},{65,1},{2,66},{66,2},{3,67},{67,3},{4,68},{68... | collective-permute-start | bytes 1572872 | tf_op jit(solution)/shard_map/ppermute | solution.py:259
  3.4 29.9 %collective-permute-start.4 = (bf16[512,512]{1,0:T(8,128)(2,1)}, bf16[512,512]{1,0:T(8,128)(2,1)}, u32[]{:S(2)}, u32[]{:S(2)}) collective-permute-start(bf16[512,512]{1,0:T(8,128)(2,1)} %bitcast.355), channel_id=1, source_target_pairs={{0,64},{64,0},{1,65},{65,1},{2,66},{66,2},{3,67},{67,3},{4,68},{68... | collective-permute-start | bytes 1572872 | tf_op jit(solution)/shard_map/ppermute | solution.py:259
  3.5 32.7 %collective-permute-start.2 = (bf16[512,1536]{1,0:T(8,128)(2,1)}, bf16[512,1536]{1,0:T(8,128)(2,1)}, u32[]{:S(2)}, u32[]{:S(2)}) collective-permute-start(bf16[512,1536]{1,0:T(8,128)(2,1)} %bitcast.339), channel_id=1, source_target_pairs={{0,64},{64,0},{1,65},{65,1},{2,66},{66,2},{3,67},{67,3},{4,68},{68... | collective-permute-start | bytes 4718600 | tf_op jit(solution)/shard_map/ppermute | solution.py:259
  11.9 0.9 copy-start.7
  12.0 21.1 %copy-start.10 = (bf16[2,256,512]{2,1,0:T(8,128)(2,1)}, bf16[2,256,512]{2,1,0:T(8,128)(2,1)S(1)}, u32[]{:S(2)}) copy-start(bf16[2,256,512]{2,1,0:T(8,128)(2,1)S(1)} %get-tuple-element.77) | copy-start | bytes 1572868
  32.4 1.0 copy-start.23
  33.4 2.7 %copy-start.20 = (bf16[1,512,1536]{2,1,0:T(8,128)(2,1)S(1)}, bf16[1,512,1536]{2,1,0:T(8,128)(2,1)}, u32[]{:S(2)}) copy-start(bf16[1,512,1536]{2,1,0:T(8,128)(2,1)} %param.9) | copy-start | bytes 4718596
  37.8 2.8 %copy-start = (bf16[512,1536]{1,0:T(8,128)(2,1)}, bf16[512,1536]{1,0:T(8,128)(2,1)S(1)}, u32[]{:S(2)}) copy-start(bf16[512,1536]{1,0:T(8,128)(2,1)S(1)} %get-tuple-element.75) | copy-start | bytes 4718596
  37.8 45.3 %copy-start.3 = (bf16[512,1536]{1,0:T(8,128)(2,1)}, bf16[512,1536]{1,0:T(8,128)(2,1)S(1)}, u32[]{:S(2)}) copy-start(bf16[512,1536]{1,0:T(8,128)(2,1)S(1)} %get-tuple-element.74) | copy-start | bytes 4718596
  38.4 1.3 copy-start.12
  39.7 0.9 copy-start.13
  40.6 0.9 copy-start.14
  41.5 0.9 copy-start.15
  41.5 1.4 slice-start
  83.1 1.3 copy-start.16
  85.1 2.8 %slice-start.1 = ((bf16[256,1536]{1,0:T(8,128)(2,1)}), bf16[256,1024]{1,0:T(8,128)(2,1)S(1)}, s32[]{:S(2)}) async-start(bf16[256,1536]{1,0:T(8,128)(2,1)} %copy-done.13), calls=%async_computation.1 | async-start | bytes 1048576 | tf_op jit(solution)/shard_map/slice | solution.py:281
  120.0 1.8 copy-start.4
  120.2 2.9 %copy-start.17 = (bf16[512,1024]{1,0:T(8,128)(2,1)}, bf16[512,1024]{1,0:T(8,128)(2,1)S(1)}, u32[]{:S(2)}) copy-start(bf16[512,1024]{1,0:T(8,128)(2,1)S(1)} %maximum_convert_fusion.1) | copy-start | bytes 3145732
  125.0 2.0 copy-start.5
  125.0 2.0 copy-start.8
  125.0 2.0 slice-start.4
  127.0 1.0 copy-start.22
  127.0 1.2 slice-start.3
  130.0 1.3 copy-start.24
  162.7 1.4 copy-start.1
  164.1 1.0 copy-start.18
  167.0 2.0 slice-start.5
  168.7 1.4 copy-start.6
  168.7 1.5 copy-start.9
  170.2 1.0 slice-start.2
  173.1 1.3 copy-start.25
  202.2 1.4 copy-start.2
  203.6 1.0 copy-start.19
  205.8 20.0 %slice-start.7 = ((bf16[512,1024]{1,0:T(8,128)(2,1)}), bf16[256,1024]{1,0:T(8,128)(2,1)S(1)}, s32[]{:S(2)}) async-start(bf16[512,1024]{1,0:T(8,128)(2,1)} %copy-done.19), calls=%async_computation.7 | async-start | bytes 1048576 | tf_op jit(solution)/shard_map/slice | solution.py:310
  225.8 1.0 copy-start.11
  225.8 1.2 slice-start.6
  228.7 4.0 %collective-permute-start.5 = (bf16[2,256,512]{2,1,0:T(8,128)(2,1)S(1)}, bf16[2,256,512]{2,1,0:T(8,128)(2,1)S(1)}, u32[]{:S(2)}, u32[]{:S(2)}) collective-permute-start(bf16[2,256,512]{2,1,0:T(8,128)(2,1)S(1)} %pad_maximum_fusion.7), channel_id=1, source_target_pairs={{0,64},{64,0},{1,65},{65,1},{2,66},{66,2},{3,67},{67,3},{4,68},{68... | collective-permute-start | bytes 1572872 | tf_op jit(solution)/shard_map/ppermute | solution.py:259

commit v7 on v5

--- a/solution.py
+++ b/solution.py
@@ -351,7 +351,11 @@
         )
     )
     params = [
-        [pick(own_part, got_part, core, section) for own_part, got_part in zip(own, got)]
+        list(
+            lax.optimization_barrier(
+                tuple(pick(own_part, got_part, core, section) for own_part, got_part in zip(own, got))
+            )
+        )
         for section in range(sections)
     ]
     cotangent_mine = mine(cotangent, core)

time: 237 us -> 242 us (1.021)
  other arithmetic: 18.4 us -> 22.3 us
  Pallas kernels: 164 us -> 167 us
    pallas_call x6, Pallas kernels: 164 us -> 167 us  [fused_step(): pl.pallas_call(functools.partial(fused_kernel, tuple(spreads), bool(atten...]
    unnamed x54 -> x60, local copies, waits for them, and re-layouts: 10.8 us -> 9.12 us
  transfers between devices with their start and end apart: 6 -> 6, of which waited for: 1 -> 3; matrix products, arithmetic and copies ran while one was open for 5% -> 3% of each run, Pallas kernels for 9% -> 0%
where the time goes in v7:
time: 242 us; the launch traced here: 238 us
  Pallas kernels  167 us (69%)
  local copies, waits for them, and re-layouts  23.4 us (10%)
  other arithmetic  22.3 us (9%)
  matrix products  16.8 us (7%)
  starting transfers between devices  5.01 us (2%)
    pallas_call x6, Pallas kernels, fused_step(): pl.pallas_call(functools.partial(fused_kernel, tuple(spreads), bool(atten...  167 us
    unnamed x60, local copies, waits for them, and re-layouts  9.12 us
    dot_general x4, matrix products, attach(): jnp.dot(fetched, weight_in[:, model_width:], preferred_element_type=jnp.f...  6.92 us
    gather x4, local copies, waits for them, and re-layouts, attach(): jnp.take(received, unit['window_at'], axis=0).reshape(-1, model_width)  5.39 us
    ppermute x6, starting transfers between devices, swap_cores(): return lax.ppermute(value, 'pipe', [(0, 1), (1, 0)])  5.01 us
    eq x8, other arithmetic, outgoing(): slots == unit['window_at'][entry]  4.89 us
  transfers between devices with their start and end apart: 6, of which 3 were waited for; matrix products, arithmetic and copies ran while one was open for 3% of the time, Pallas kernels for 0%

profile of v7, /device:TPU:15, one launch (start us, length us, event | category | flops | bytes accessed | tf_op | source)
XLA Modules:
  0.0 238.0 jit_solution(16696594532088054473)
XLA Ops:
  0.0 0.7 collective-permute-start.2
  0.7 1.1 dynamic-slice_bitcast_fusion
  1.9 0.8 reshape_squeeze.9
  2.8 0.5 collective-permute-start.1
  4.0 0.5 collective-permute-done.1
  4.7 0.7 broadcast_select_fusion.9
  5.4 1.1 bitcast_select_fusion.9
  6.6 2.5 %broadcast_select_fusion.3 = (bf16[512,512]{1,0:T(8,128)(2,1)}, bf16[512,512]{1,0:T(8,128)(2,1)}) fusion(bf16[512,512]{1,0:T(8,128)(2,1)} %collective-permute-done.3, pred[]{:T(512)S(6)} %eq.114, bf16[1,512,512]{2,1,0:T(8,128)(2,1)S(1)} %copy-done.28, pred[]{:T(512)S(6)} %eq.113), kind=kLoop, calls=%fused_computation.163 | loop fusion | flops 524288 | bytes 2097154 | tf_op jit(solution)/shard_map/jit(_where)/select_n | solution.py:262
  9.3 0.7 fusion.133
  10.1 0.8 fusion.131
  11.6 0.6 convolution_convert_fusion
  12.3 0.6 convolution_convert_fusion.1
  14.1 0.6 convolution_convert_fusion.2
  14.7 0.6 convolution_convert_fusion.3
  15.6 0.9 slice.241
  16.5 19.2 %shard_map.64 = bf16[4,256,512]{2,1,0:T(8,128)(2,1)S(1)} custom-call(bf16[256,512]{1,0:T(8,128)(2,1)S(1)} %get-tuple-element.109.refs_0_), custom_call_target="tpu_custom_call" | custom-call | bytes 1048577 | tf_op jit(solution)/shard_map/pallas_call | solution.py:236
  35.7 1.3 gather_fusion
  37.0 1.1 broadcast_select_fusion.7
  38.1 1.7 convolution_convert_fusion.7
  40.3 43.2 %shard_map.65 = (f32[256,512]{1,0:T(8,128)S(1)}, f32[512,512]{1,0:T(8,128)S(1)}, f32[512,512]{1,0:T(8,128)S(1)}, bf16[4,256,512]{2,1,0:T(8,128)(2,1)S(1)}, bf16[...) custom-call(bf16[256,512]{1,0:T(8,128)(2,1)S(1)} %slice.240.refs_0_, ...), custom_call_target="tpu_custom_call" | custom-call | flops 5368709120 | bytes 3145729 | tf_op jit(solution)/shard_map/pallas_call | solution.py:236
  83.6 1.3 copy-done.4
  84.9 0.5 fusion.32
  85.4 0.5 copy-done.19
  85.9 0.6 fusion.104
  86.6 0.6 fusion.105
  87.6 0.6 gather_fusion.1
  88.3 1.7 convolution_convert_fusion.6
  90.7 1.2 fusion.7.refs_4_
  91.9 29.9 %shard_map.66 = (f32[256,512]{1,0:T(8,128)S(1)}, f32[512,512]{1,0:T(8,128)S(1)}, f32[512,512]{1,0:T(8,128)S(1)}, bf16[4,256,512]{2,1,0:T(8,128)(2,1)S(1)}) custom-call(bf16[256,512]{1,0:T(8,128)(2,1)S(1)} %slice.245.refs_0_, bf16[512,512]{1,0:T(8,128)(2,1)S(1)} %get-tuple-element.99.refs_1_, bf16[512,512]{1,0:T(8,128)(2,1)S(1)} %get-tuple-element.98.refs_2_, ...), custom_call_target="tpu_custom_call" | custom-call | flops 5368709120 | bytes 4194305 | tf_op jit(solution)/shard_map/pallas_call | solution.py:236
  122.0 1.6 copy-done.5
  123.6 1.3 fusion.30
  124.9 0.6 fusion.103
  125.6 0.6 fusion.102
  126.2 0.7 convert.32
  127.0 1.8 gather_fusion.2
  128.9 1.8 convolution_convert_fusion.5
  131.0 0.7 fusion.120
  132.2 1.2 fusion.47
  134.4 1.2 fusion.5.refs_4_
  135.6 26.3 %shard_map.67 = (f32[256,512]{1,0:T(8,128)S(1)}, f32[512,512]{1,0:T(8,128)S(1)}, f32[512,512]{1,0:T(8,128)S(1)}, bf16[4,256,512]{2,1,0:T(8,128)(2,1)S(1)}) custom-call(bf16[256,512]{1,0:T(8,128)(2,1)S(1)} %slice.252.refs_0_, bf16[512,512]{1,0:T(8,128)(2,1)S(1)} %get-tuple-element.101.refs_1_, bf16[512,512]{1,0:T(8,128)(2,1)S(1)} %get-tuple-element.100.refs_2_, ...), custom_call_target="tpu_custom_call" | custom-call | flops 5368709120 | bytes 4194305 | tf_op jit(solution)/shard_map/pallas_call | solution.py:236
  162.1 1.3 copy-done.1
  163.4 1.3 fusion.26
  164.6 0.6 fusion.100
  165.3 0.7 fusion.101
  166.1 1.8 gather_fusion.3
  168.0 1.7 convolution_convert_fusion.4
  169.9 1.2 copy-done.7
  171.2 0.7 fusion.119
  171.9 1.3 fusion.60
  174.3 1.2 fusion.3.refs_4_
  175.5 29.9 %shard_map.68 = (f32[256,512]{1,0:T(8,128)S(1)}, f32[512,512]{1,0:T(8,128)S(1)}, f32[512,512]{1,0:T(8,128)S(1)}, bf16[4,256,512]{2,1,0:T(8,128)(2,1)S(1)}) custom-call(bf16[256,512]{1,0:T(8,128)(2,1)S(1)} %slice.260.refs_0_, bf16[512,512]{1,0:T(8,128)(2,1)S(1)} %get-tuple-element.97.refs_1_, bf16[512,512]{1,0:T(8,128)(2,1)S(1)} %get-tuple-element.96.refs_2_, ...), custom_call_target="tpu_custom_call" | custom-call | flops 5368709120 | bytes 4194305 | tf_op jit(solution)/shard_map/pallas_call | solution.py:236
  205.6 1.3 copy-done.2
  206.9 0.5 fusion.24
  207.3 0.5 copy-done.22
  207.8 0.6 fusion.99
  208.5 0.6 fusion.98
  210.0 0.5 fusion.1.refs_0_
  210.5 18.5 %shard_map.69 = bf16[4,256,512]{2,1,0:T(8,128)(2,1)S(1)} custom-call(bf16[4,256,512]{2,1,0:T(8,128)(2,1)S(1)} %fusion.1.refs_0_), custom_call_target="tpu_custom_call" | custom-call | bytes 4194305 | tf_op jit(solution)/shard_map/pallas_call | solution.py:236
  229.2 0.6 fusion.8
  230.3 0.8 fusion.118
  231.2 0.7 select_bitcast_fusion.5
  232.0 3.2 %collective-permute-start.5 = (bf16[2,256,512]{2,1,0:T(8,128)(2,1)S(1)}, bf16[2,256,512]{2,1,0:T(8,128)(2,1)S(1)}, u32[]{:S(2)}, u32[]{:S(2)}) collective-permute-start(bf16[2,256,512]{2,1,0:T(8,128)(2,1)S(1)} %pad_maximum_fusion.6), channel_id=1, source_target_pairs={{0,64},{64,0},{1,65},{65,1},{2,66},{66,2},{3,67},{67,3},{4,68},{68... | collective-permute-start | bytes 1572872 | tf_op jit(solution)/shard_map/ppermute | solution.py:258
  235.2 1.5 collective-permute-done.5
  236.9 1.0 copy.15
  (158 shorter events, 11.1 us)
Async XLA Ops:
  0.0 9.1 %collective-permute-start.2 = (bf16[512,1536]{1,0:T(8,128)(2,1)}, bf16[512,1536]{1,0:T(8,128)(2,1)S(1)}, u32[]{:S(2)}, u32[]{:S(2)}) collective-permute-start(bf16[512,1536]{1,0:T(8,128)(2,1)} %bitcast.329), channel_id=1, source_target_pairs={{0,64},{64,0},{1,65},{65,1},{2,66},{66,2},{3,67},{67,3},{4,68},{68... | collective-permute-start | bytes 4718600 | tf_op jit(solution)/shard_map/ppermute | solution.py:258
  0.7 5.9 %copy-start.28 = (bf16[1,512,512]{2,1,0:T(8,128)(2,1)S(1)}, bf16[1,512,512]{2,1,0:T(8,128)(2,1)}, u32[]{:S(2)}) copy-start(bf16[1,512,512]{2,1,0:T(8,128)(2,1)} %param.10) | copy-start | bytes 1572868
  1.8 3.6 %collective-permute-start = (bf16[2,256,512]{2,1,0:T(8,128)(2,1)S(1)}, bf16[2,256,512]{2,1,0:T(8,128)(2,1)S(1)}, u32[]{:S(2)}, u32[]{:S(2)}) collective-permute-start(bf16[2,256,512]{2,1,0:T(8,128)(2,1)S(1)} %dynamic-slice_bitcast_fusion), channel_id=1, source_target_pairs={{0,64},{64,0},{1,65},{65,1},{2,66},{66,2},{3,67},{67,3},{4,68},{68... | collective-permute-start | bytes 1572872 | tf_op jit(solution)/shard_map/ppermute | solution.py:258
  2.8 1.6 collective-permute-start.1
  3.3 1.4 collective-permute-start.4
  3.4 3.1 %collective-permute-start.3 = (bf16[512,512]{1,0:T(8,128)(2,1)}, bf16[512,512]{1,0:T(8,128)(2,1)}, u32[]{:S(2)}, u32[]{:S(2)}) collective-permute-start(bf16[512,512]{1,0:T(8,128)(2,1)} %bitcast.336), channel_id=1, source_target_pairs={{0,64},{64,0},{1,65},{65,1},{2,66},{66,2},{3,67},{67,3},{4,68},{68... | collective-permute-start | bytes 1572872 | tf_op jit(solution)/shard_map/ppermute | solution.py:258
  6.5 4.9 %copy-start.10 = (bf16[2,256,512]{2,1,0:T(8,128)(2,1)}, bf16[2,256,512]{2,1,0:T(8,128)(2,1)S(1)}, u32[]{:S(2)}) copy-start(bf16[2,256,512]{2,1,0:T(8,128)(2,1)S(1)} %get-tuple-element.39) | copy-start | bytes 1572868
  6.5 7.2 %copy-start.8 = (bf16[2,256,512]{2,1,0:T(8,128)(2,1)}, bf16[2,256,512]{2,1,0:T(8,128)(2,1)S(1)}, u32[]{:S(2)}) copy-start(bf16[2,256,512]{2,1,0:T(8,128)(2,1)S(1)} %get-tuple-element.34) | copy-start | bytes 1572868
  6.5 2.5 %copy-start.24 = (bf16[1,512,1536]{2,1,0:T(8,128)(2,1)S(1)}, bf16[1,512,1536]{2,1,0:T(8,128)(2,1)}, u32[]{:S(2)}) copy-start(bf16[1,512,1536]{2,1,0:T(8,128)(2,1)} %param.9) | copy-start | bytes 4718596
  9.3 3.0 %copy-start = (bf16[512,1536]{1,0:T(8,128)(2,1)}, bf16[512,1536]{1,0:T(8,128)(2,1)S(1)}, u32[]{:S(2)}) copy-start(bf16[512,1536]{1,0:T(8,128)(2,1)S(1)} %get-tuple-element.46) | copy-start | bytes 4718596
  9.3 5.4 %copy-start.3 = (bf16[512,1536]{1,0:T(8,128)(2,1)}, bf16[512,1536]{1,0:T(8,128)(2,1)S(1)}, u32[]{:S(2)}) copy-start(bf16[512,1536]{1,0:T(8,128)(2,1)S(1)} %get-tuple-element.36) | copy-start | bytes 4718596
  12.2 0.9 copy-start.16
  13.2 1.0 copy-start.17
  14.7 0.9 copy-start.18
  35.7 4.2 %copy-start.14 = (bf16[512,512]{1,0:T(8,128)(2,1)S(1)}, bf16[512,512]{1,0:T(8,128)(2,1)}, u32[]{:S(2)}) copy-start(bf16[512,512]{1,0:T(8,128)(2,1)} %get-tuple-element.38) | copy-start | bytes 1572868
  37.0 2.9 %copy-start.25 = (bf16[4,256,512]{2,1,0:T(8,128)(2,1)S(1)}, bf16[4,256,512]{2,1,0:T(8,128)(2,1)}, u32[]{:S(2)}) copy-start(bf16[4,256,512]{2,1,0:T(8,128)(2,1)} %param.13) | copy-start | bytes 3145732
  38.1 2.1 copy-start.23
  83.5 1.4 copy-start.4
  84.9 1.0 copy-start.19
  84.9 2.3 copy-start.15
  88.3 1.8 slice-start.2
  121.9 1.8 copy-start.5
  122.0 2.9 %copy-start.20 = (bf16[512,1024]{1,0:T(8,128)(2,1)}, bf16[512,1024]{1,0:T(8,128)(2,1)S(1)}, u32[]{:S(2)}) copy-start(bf16[512,1024]{1,0:T(8,128)(2,1)S(1)} %maximum_convert_fusion.1) | copy-start | bytes 3145732
  128.9 2.0 copy-start.6
  128.9 2.0 copy-start.9
  128.9 2.0 slice-start.3
  128.9 2.0 copy-start.29
  130.9 1.0 copy-start.27
  131.0 1.2 slice-start.1
  132.1 1.3 copy-start.12
  161.9 1.4 copy-start.1
  163.4 1.3 copy-start.21
  169.7 1.4 copy-start.7
  169.7 1.5 slice-start.4
  171.2 2.1 copy-start.13
  171.9 1.7 copy-start.26
  171.9 1.7 slice-start
  205.4 1.4 copy-start.2
  206.9 1.0 copy-start.22
  210.4 18.7 %slice-start.6 = ((bf16[512,1024]{1,0:T(8,128)(2,1)}), bf16[256,1024]{1,0:T(8,128)(2,1)S(1)}, s32[]{:S(2)}) async-start(bf16[512,1024]{1,0:T(8,128)(2,1)} %copy-done.22), calls=%async_computation.6 | async-start | bytes 1048576 | tf_op jit(solution)/shard_map/slice | solution.py:309
  229.1 1.0 copy-start.11
  229.1 1.2 slice-start.5
  232.0 4.8 %collective-permute-start.5 = (bf16[2,256,512]{2,1,0:T(8,128)(2,1)S(1)}, bf16[2,256,512]{2,1,0:T(8,128)(2,1)S(1)}, u32[]{:S(2)}, u32[]{:S(2)}) collective-permute-start(bf16[2,256,512]{2,1,0:T(8,128)(2,1)S(1)} %pad_maximum_fusion.6), channel_id=1, source_target_pairs={{0,64},{64,0},{1,65},{65,1},{2,66},{66,2},{3,67},{67,3},{4,68},{68... | collective-permute-start | bytes 1572872 | tf_op jit(solution)/shard_map/ppermute | solution.py:258

commit v8 on v5

--- a/solution.py
+++ b/solution.py
@@ -211,7 +211,8 @@
             hooks[heads // 2] = functools.partial(relay, list(range(count)))
         attention_body(*attention_in, *attention_out, hooks)
     else:
-        relay(list(range(count)))
+        for which in range(count):
+            relay([which])
     finish()
 
 
@@ -362,8 +363,10 @@
     ]
     results = {}
     ids = iter(range(len(order) + 2))
-    (first_received,) = fused_step((), [units[0]["normed"]], [False], next(ids))
-    attach(units[0], first_received, params[order[0][0]][2])
+    early = min(2, len(units))
+    first_received = fused_step((), [unit["normed"] for unit in units[:early]], [False] * early, next(ids))
+    for unit, (unit_section, _), arrived in zip(units[:early], order[:early], first_received):
+        attach(unit, arrived, params[unit_section][2])
     pending = None
     for step, (section, j) in enumerate(order):
         unit = units[step]
@@ -378,7 +381,7 @@
             payloads.append(pending[1])
             spreads.append(True)
         if step == 0:
-            for later in units[1:]:
+            for later in units[early:]:
                 payloads.append(later["normed"])
                 spreads.append(False)
         outs = fused_step(
@@ -403,7 +406,7 @@
             )
             received = received[1:]
         if step == 0:
-            for later, (later_section, _), arrived in zip(units[1:], order[1:], received):
+            for later, (later_section, _), arrived in zip(units[early:], order[early:], received):
                 attach(later, arrived, params[later_section][2])
         unit["grad_query"] = grad_query
         pending = (step, outgoing(unit, grad_key, grad_value, weight_in))

time: 237 us -> 232 us (0.979)
  local copies, waits for them, and re-layouts: 24.5 us -> 21.9 us
  transfers between devices with their start and end apart: 6 -> 6, of which waited for: 1 -> 1; matrix products, arithmetic and copies ran while one was open for 5% -> 5% of each run, Pallas kernels for 9% -> 13%
where the time goes in v8:
time: 232 us; the launch traced here: 229 us
  Pallas kernels  165 us (71%)
  local copies, waits for them, and re-layouts  21.9 us (9%)
  other arithmetic  19.1 us (8%)
  matrix products  15.6 us (7%)
  starting transfers between devices  4.11 us (2%)
    pallas_call x6, Pallas kernels, fused_step(): pl.pallas_call(functools.partial(fused_kernel, tuple(spreads), bool(atten...  165 us
    unnamed x54, local copies, waits for them, and re-layouts  9.85 us
    eq x8, other arithmetic, outgoing(): slots == unit['window_at'][entry]  5.11 us
  transfers between devices with their start and end apart: 6, of which 1 were waited for; matrix products, arithmetic and copies ran while one was open for 5% of the time, Pallas kernels for 13%

profile of v8, /device:TPU:15, one launch (start us, length us, event | category | flops | bytes accessed | tf_op | source)
XLA Modules:
  0.0 228.8 jit_solution(1252848362581290660)
XLA Ops:
  0.0 0.8 reshape_squeeze.9
  1.0 0.7 collective-permute-start.3
  1.8 1.1 dynamic-slice_bitcast_fusion
  2.9 0.5 collective-permute-start
  4.0 0.7 fusion.137
  4.7 0.6 fusion.135
  5.4 0.7 fusion.103
  6.1 0.6 fusion.102
  6.8 0.6 fusion.104
  7.5 0.6 fusion.105
  8.2 0.6 fusion.99
  9.0 0.7 fusion.98
  9.7 0.6 fusion.100
  10.3 0.7 fusion.101
  11.2 0.7 broadcast_select_fusion.13
  13.1 30.3 %shard_map.64 = (bf16[4,256,512]{2,1,0:T(8,128)(2,1)S(1)}, bf16[4,256,512]{2,1,0:T(8,128)(2,1)S(1)}) custom-call(bf16[256,512]{1,0:T(8,128)(2,1)S(1)} %get-tuple-element.89.refs_0_, bf16[256,512]{1,0:T(8,128)(2,1)S(1)} %get-tuple-element.88.refs_1_), custom_call_target="tpu_custom_call" | custom-call | bytes 2097153 | tf_op jit(solution)/shard_map/pallas_call | solution.py:237
  43.5 0.6 gather_fusion
  44.2 0.6 gather_fusion.1
  45.1 0.8 copy-done.23
  46.8 0.7 copy-done.19
  47.5 1.6 broadcast_select_fusion.1
  49.2 0.6 convolution_convert_fusion.2
  49.8 0.6 convolution_convert_fusion.3
  50.3 0.7 copy-done.11
  51.1 0.6 convolution_convert_fusion
  52.0 0.6 convolution_convert_fusion.1
  52.8 0.8 copy-done.14
  54.2 29.9 %shard_map.65 = (f32[256,512]{1,0:T(8,128)S(1)}, f32[512,512]{1,0:T(8,128)S(1)}, f32[512,512]{1,0:T(8,128)S(1)}, bf16[4,256,512]{2,1,0:T(8,128)(2,1)S(1)}, bf16[4,256,512]{2,1,0:T(8,128)(2,1)}) custom-call(bf16[256,512]{1,0:T(8,128)(2,1)S(1)} %slice.241.refs_0_, bf16[512,512]{1,0:T(8,128)(2,1)S(1)} %get-tuple-element.85.refs_1_, ...), custom_call_target="tpu_custom_call" | custom-call | flops 5368709120 | bytes 2097153 | tf_op jit(solution)/shard_map/pallas_call | solution.py:237
  84.3 0.5 fusion.32
  84.8 0.5 copy-done.15
  85.8 0.6 slice-done
  86.9 1.2 fusion.7.refs_4_
  88.2 28.5 %shard_map.66 = (f32[256,512]{1,0:T(8,128)S(1)}, f32[512,512]{1,0:T(8,128)S(1)}, f32[512,512]{1,0:T(8,128)S(1)}, bf16[4,256,512]{2,1,0:T(8,128)(2,1)S(1)}) custom-call(bf16[256,512]{1,0:T(8,128)(2,1)S(1)} %slice.250.refs_0_, bf16[512,512]{1,0:T(8,128)(2,1)S(1)} %get-tuple-element.81.refs_1_, bf16[512,512]{1,0:T(8,128)(2,1)S(1)} %get-tuple-element.80.refs_2_, ...), custom_call_target="tpu_custom_call" | custom-call | flops 5368709120 | bytes 4194305 | tf_op jit(solution)/shard_map/pallas_call | solution.py:237
  116.8 1.3 fusion.30
  118.1 0.7 convert.32
  118.8 0.6 gather_fusion.2
  119.5 1.8 convolution_convert_fusion.5
  121.5 0.7 fusion.124
  122.8 1.2 fusion.47
  124.5 1.2 fusion.5.refs_4_
  125.8 1.4 convolution_convert_fusion.9.refs_3_
  127.2 27.9 %shard_map.67 = (f32[256,512]{1,0:T(8,128)S(1)}, f32[512,512]{1,0:T(8,128)S(1)}, f32[512,512]{1,0:T(8,128)S(1)}, bf16[4,256,512]{2,1,0:T(8,128)(2,1)S(1)}) custom-call(bf16[256,512]{1,0:T(8,128)(2,1)S(1)} %slice.257.refs_0_, bf16[512,512]{1,0:T(8,128)(2,1)S(1)} %get-tuple-element.83.refs_1_, bf16[512,512]{1,0:T(8,128)(2,1)S(1)} %get-tuple-element.82.refs_2_, ...), custom_call_target="tpu_custom_call" | custom-call | flops 5368709120 | bytes 4194305 | tf_op jit(solution)/shard_map/pallas_call | solution.py:237
  155.2 1.3 copy-done.1
  156.5 0.5 fusion.26
  156.9 0.5 copy-done.17
  157.5 1.8 gather_fusion.3
  159.4 1.7 convolution_convert_fusion.4
  161.3 1.2 copy-done.5
  162.6 0.7 fusion.123
  163.7 1.2 fusion.60
  165.5 1.2 fusion.3.refs_4_
  166.7 1.4 convolution_convert_fusion.8.refs_3_
  168.1 28.5 %shard_map.68 = (f32[256,512]{1,0:T(8,128)S(1)}, f32[512,512]{1,0:T(8,128)S(1)}, f32[512,512]{1,0:T(8,128)S(1)}, bf16[4,256,512]{2,1,0:T(8,128)(2,1)S(1)}) custom-call(bf16[256,512]{1,0:T(8,128)(2,1)S(1)} %slice.266.refs_0_, bf16[512,512]{1,0:T(8,128)(2,1)S(1)} %get-tuple-element.79.refs_1_, bf16[512,512]{1,0:T(8,128)(2,1)S(1)} %get-tuple-element.78.refs_2_, ...), custom_call_target="tpu_custom_call" | custom-call | flops 5368709120 | bytes 4194305 | tf_op jit(solution)/shard_map/pallas_call | solution.py:237
  196.8 1.3 copy-done.2
  198.1 0.5 fusion.24
  198.5 0.5 copy-done.18
  199.8 0.5 fusion.1.refs_0_
  200.3 20.3 %shard_map.69 = bf16[4,256,512]{2,1,0:T(8,128)(2,1)S(1)} custom-call(bf16[4,256,512]{2,1,0:T(8,128)(2,1)S(1)} %fusion.1.refs_0_), custom_call_target="tpu_custom_call" | custom-call | bytes 4194305 | tf_op jit(solution)/shard_map/pallas_call | solution.py:237
  220.9 0.6 fusion.8
  222.0 0.8 fusion.122
  222.9 0.7 select_bitcast_fusion.5
  223.7 2.3 %collective-permute-start.5 = (bf16[2,256,512]{2,1,0:T(8,128)(2,1)S(1)}, bf16[2,256,512]{2,1,0:T(8,128)(2,1)S(1)}, u32[]{:S(2)}, u32[]{:S(2)}) collective-permute-start(bf16[2,256,512]{2,1,0:T(8,128)(2,1)S(1)} %pad_maximum_fusion.6), channel_id=1, source_target_pairs={{0,64},{64,0},{1,65},{65,1},{2,66},{66,2},{3,67},{67,3},{4,68},{68... | collective-permute-start | bytes 1572872 | tf_op jit(solution)/shard_map/ppermute | solution.py:259
  226.0 1.5 collective-permute-done.5
  227.7 1.0 copy.15
  (153 shorter events, 11.1 us)
Async XLA Ops:
  0.0 11.9 %copy-start.20 = (bf16[1,4,256,512]{3,2,1,0:T(8,128)(2,1)S(1)}, bf16[1,4,256,512]{3,2,1,0:T(8,128)(2,1)}, u32[]{:S(2)}) copy-start(bf16[1,4,256,512]{3,2,1,0:T(8,128)(2,1)} %param.8) | copy-start | bytes 3145732
  1.0 3.0 %collective-permute-start.3 = (s32[2,2]{1,0:T(2,128)S(1)}, s32[2,2]{1,0:T(2,128)S(1)}, u32[]{:S(2)}, u32[]{:S(2)}) collective-permute-start(s32[2,2]{1,0:T(2,128)S(1)} %bitcast.354), channel_id=1, source_target_pairs={{0,64},{64,0},{1,65},{65,1},{2,66},{66,2},{3,67},{67,3},{4,68},{68... | collective-permute-start | bytes 56 | tf_op jit(solution)/shard_map/ppermute | solution.py:259
  1.7 9.5 %collective-permute-start.1 = (f32[512]{0:T(512)}, f32[512]{0:T(512)S(1)}, u32[]{:S(2)}, u32[]{:S(2)}) collective-permute-start(f32[512]{0:T(512)} %bitcast.352), channel_id=1, source_target_pairs={{0,64},{64,0},{1,65},{65,1},{2,66},{66,2},{3,67},{67,3},{4,68},{68... | collective-permute-start | bytes 6152 | tf_op jit(solution)/shard_map/ppermute | solution.py:259
  2.9 9.0 %collective-permute-start = (bf16[2,256,512]{2,1,0:T(8,128)(2,1)S(1)}, bf16[2,256,512]{2,1,0:T(8,128)(2,1)S(1)}, u32[]{:S(2)}, u32[]{:S(2)}) collective-permute-start(bf16[2,256,512]{2,1,0:T(8,128)(2,1)S(1)} %dynamic-slice_bitcast_fusion), channel_id=1, source_target_pairs={{0,64},{64,0},{1,65},{65,1},{2,66},{66,2},{3,67},{67,3},{4,68},{68... | collective-permute-start | bytes 1572872 | tf_op jit(solution)/shard_map/ppermute | solution.py:259
  3.4 41.8 %collective-permute-start.4 = (bf16[512,512]{1,0:T(8,128)(2,1)}, bf16[512,512]{1,0:T(8,128)(2,1)}, u32[]{:S(2)}, u32[]{:S(2)}) collective-permute-start(bf16[512,512]{1,0:T(8,128)(2,1)} %bitcast.355), channel_id=1, source_target_pairs={{0,64},{64,0},{1,65},{65,1},{2,66},{66,2},{3,67},{67,3},{4,68},{68... | collective-permute-start | bytes 1572872 | tf_op jit(solution)/shard_map/ppermute | solution.py:259
  3.5 43.4 %collective-permute-start.2 = (bf16[512,1536]{1,0:T(8,128)(2,1)}, bf16[512,1536]{1,0:T(8,128)(2,1)}, u32[]{:S(2)}, u32[]{:S(2)}) collective-permute-start(bf16[512,1536]{1,0:T(8,128)(2,1)} %bitcast.340), channel_id=1, source_target_pairs={{0,64},{64,0},{1,65},{65,1},{2,66},{66,2},{3,67},{67,3},{4,68},{68... | collective-permute-start | bytes 4718600 | tf_op jit(solution)/shard_map/ppermute | solution.py:259
  11.9 1.2 copy-start.6
  12.0 32.9 %copy-start.9 = (bf16[2,256,512]{2,1,0:T(8,128)(2,1)}, bf16[2,256,512]{2,1,0:T(8,128)(2,1)S(1)}, u32[]{:S(2)}) copy-start(bf16[2,256,512]{2,1,0:T(8,128)(2,1)S(1)} %get-tuple-element.75) | copy-start | bytes 1572868
  44.8 1.2 copy-start.23
  44.8 1.3 copy-start.24
  46.1 1.4 copy-start.19
  49.1 2.8 %copy-start = (bf16[512,1536]{1,0:T(8,128)(2,1)}, bf16[512,1536]{1,0:T(8,128)(2,1)S(1)}, u32[]{:S(2)}) copy-start(bf16[512,1536]{1,0:T(8,128)(2,1)S(1)} %get-tuple-element.73) | copy-start | bytes 4718596
  49.1 67.6 %copy-start.3 = (bf16[512,1536]{1,0:T(8,128)(2,1)}, bf16[512,1536]{1,0:T(8,128)(2,1)S(1)}, u32[]{:S(2)}) copy-start(bf16[512,1536]{1,0:T(8,128)(2,1)S(1)} %get-tuple-element.72) | copy-start | bytes 4718596
  49.7 1.3 copy-start.11
  51.0 0.9 copy-start.12
  51.9 0.9 copy-start.13
  52.8 0.9 copy-start.14
  52.8 1.3 slice-start.1
  84.3 1.0 copy-start.15
  85.3 1.0 slice-start
  116.8 1.3 copy-start.16
  119.5 2.0 copy-start.4
  119.5 2.0 copy-start.7
  119.5 2.0 slice-start.4
  119.5 2.0 copy-start.22
  121.5 1.0 copy-start.21
  121.5 1.2 slice-start.3
  124.5 1.3 copy-start.25
  155.1 1.4 copy-start.1
  156.5 1.0 copy-start.17
  159.4 2.0 slice-start.5
  161.1 1.4 copy-start.5
  161.1 1.5 copy-start.8
  162.6 1.0 slice-start.2
  165.5 1.3 copy-start.26
  196.7 1.4 copy-start.2
  198.1 1.0 copy-start.18
  200.3 20.5 %slice-start.7 = ((bf16[512,1024]{1,0:T(8,128)(2,1)}), bf16[256,1024]{1,0:T(8,128)(2,1)S(1)}, s32[]{:S(2)}) async-start(bf16[512,1024]{1,0:T(8,128)(2,1)} %copy-done.18), calls=%async_computation.7 | async-start | bytes 1048576 | tf_op jit(solution)/shard_map/slice | solution.py:310
  220.8 1.0 copy-start.10
  220.8 1.2 slice-start.6
  223.7 3.9 %collective-permute-start.5 = (bf16[2,256,512]{2,1,0:T(8,128)(2,1)S(1)}, bf16[2,256,512]{2,1,0:T(8,128)(2,1)S(1)}, u32[]{:S(2)}, u32[]{:S(2)}) collective-permute-start(bf16[2,256,512]{2,1,0:T(8,128)(2,1)S(1)} %pad_maximum_fusion.6), channel_id=1, source_target_pairs={{0,64},{64,0},{1,65},{65,1},{2,66},{66,2},{3,67},{67,3},{4,68},{68... | collective-permute-start | bytes 1572872 | tf_op jit(solution)/shard_map/ppermute | solution.py:259
